TPU v7x, 256 devices: a whole 4x4x8 slice. The times are simulated.
256 devices in a mesh: dp: 16 (over y, z_lo, core), owner: 16 (over x, z_hi).
Axes of the slice: x: 4, y: 4, z: 8 (z_hi: 4, z_lo: 2; z = z_hi * 2 + z_lo), core: 2. Of those that a mesh axis runs over, the one named last changes fastest.
Arguments:
- tokens: bfloat16 [8192, 4096], P('dp'), may hold values from -6 to 6
- route: int32 [8192, 1], P('dp'), may hold values from 0 to 3; in each aligned block of 512 rows (0 to 511, 512 to 1023, ...) at most 384 rows name the same one
- gate_prob: float32 [8192], P('dp'), may hold values from 0.1 to 1
- w_gate: bfloat16 [4096, 6144], P('dp', 'owner'), may hold values from -0.09375 to 0.09375
- w_up: bfloat16 [4096, 6144], P('dp', 'owner'), may hold values from -0.09375 to 0.09375
- w_down: bfloat16 [6144, 4096], P('owner', 'dp'), may hold values from -0.15625 to 0.15625
- d_out: bfloat16 [8192, 4096], P('dp', 'owner'), may hold values from -1.5 to 1.5
Outputs:
- mixed: bfloat16 [8192, 4096], P('dp', 'owner')
- grad_tokens: bfloat16 [8192, 4096], P('dp', 'owner')
- grad_gate: float32 [8192], P('dp')
- grad_w_gate: float32 [4096, 6144], P('dp', 'owner')
- grad_w_up: float32 [4096, 6144], P('dp', 'owner')
- grad_w_down: float32 [6144, 4096], P('owner', 'dp')
Inputs may be any that keep to these rules, and one draw needn't show every extreme that they name: `route`: in every aligned block of 512 rows no expert is named by more than 384 rows, and in some block one expert is named by exactly 384 rows.
All inputs are finite; a program needn't handle non-finite values.
Results may differ from a plain program's by a relative error of at most 0.017.
Values may be sent and summed in bfloat16 or wider, within the bound.
A program may use at most 128 MiB of HBM per device.

v0:
```python
import jax
import jax.numpy as jnp
from jax import lax
from jax.sharding import PartitionSpec as P

EXPERTS = 4


def contract_rows(left, right):
    return lax.dot_general(
        left, right, (((0,), (0,)), ((), ())), preferred_element_type=jnp.float32
    )


def contract_cols(left, right):
    return lax.dot_general(
        left, right, (((1,), (1,)), ((), ())), preferred_element_type=jnp.float32
    )


def local(tokens, route, gate_prob, w_gate, w_up, w_down, d_out):
    row_count = tokens.shape[0]
    capacity = 3 * row_count // 4
    pieces = lax.axis_size("owner") // EXPERTS
    expert = lax.axis_index("owner") // pieces
    full_gate, full_up, full_down = (
        lax.all_gather(w_gate, "dp", axis=0, tiled=True),
        lax.all_gather(w_up, "dp", axis=0, tiled=True),
        lax.all_gather(w_down, "dp", axis=1, tiled=True),
    )
    selected = route[:, 0] == expert
    slot_index = jnp.cumsum(selected.astype(jnp.int32)) - 1
    safe_index = jnp.maximum(slot_index, 0)
    slot_ids = jnp.arange(capacity, dtype=jnp.int32)
    one_hot = jnp.logical_and(slot_index[None, :] == slot_ids[:, None], selected[None, :])
    dispatch = one_hot.astype(jnp.bfloat16)
    slot_tokens = jnp.dot(dispatch, tokens, preferred_element_type=jnp.float32).astype(jnp.bfloat16)
    slot_probs = jnp.sum(jnp.where(one_hot, gate_prob[None, :], jnp.float32(0.0)), axis=1)
    row_weights = jnp.where(selected, gate_prob, jnp.float32(0.0))
    gate_pre = jnp.dot(slot_tokens, full_gate, preferred_element_type=jnp.float32)
    up_pre = jnp.dot(slot_tokens, full_up, preferred_element_type=jnp.float32)
    sigma = jax.nn.sigmoid(gate_pre)
    active = gate_pre * sigma
    hidden = (active * up_pre).astype(jnp.bfloat16)
    expert_out = jnp.dot(hidden, full_down, preferred_element_type=jnp.float32)
    row_terms = jnp.take(expert_out, safe_index, axis=0) * row_weights[:, None]
    mixed = lax.psum_scatter(
        row_terms.astype(jnp.bfloat16), "owner", scatter_dimension=1, tiled=True
    )
    d_full = lax.all_gather(d_out, "owner", axis=1, tiled=True)
    slot_cotangent = jnp.dot(dispatch, d_full, preferred_element_type=jnp.float32)
    slot_router = jnp.sum(slot_cotangent * expert_out, axis=1)
    router_terms = jnp.where(selected, jnp.take(slot_router, safe_index), jnp.float32(0.0))
    grad_gate = lax.psum(router_terms, "owner")
    d_expert = (slot_probs[:, None] * slot_cotangent).astype(jnp.bfloat16)
    d_hidden = contract_cols(d_expert, full_down)
    d_gate_pre = (d_hidden * up_pre * sigma * (1.0 + gate_pre * (1.0 - sigma))).astype(jnp.bfloat16)
    d_up_pre = (d_hidden * active).astype(jnp.bfloat16)
    slot_input = contract_cols(d_gate_pre, full_gate) + contract_cols(d_up_pre, full_up)
    input_terms = jnp.where(
        selected[:, None], jnp.take(slot_input, safe_index, axis=0), jnp.float32(0.0)
    )
    grad_tokens = lax.psum_scatter(
        input_terms.astype(jnp.bfloat16), "owner", scatter_dimension=1, tiled=True
    )
    gate_term = contract_rows(slot_tokens, d_gate_pre)
    up_term = contract_rows(slot_tokens, d_up_pre)
    down_term = contract_rows(hidden, d_expert)
    grad_w_gate, grad_w_up, grad_w_down = (
        lax.psum_scatter(
            gate_term.astype(jnp.bfloat16), "dp", scatter_dimension=0, tiled=True
        ).astype(jnp.float32),
        lax.psum_scatter(
            up_term.astype(jnp.bfloat16), "dp", scatter_dimension=0, tiled=True
        ).astype(jnp.float32),
        lax.psum_scatter(
            down_term.astype(jnp.bfloat16), "dp", scatter_dimension=1, tiled=True
        ).astype(jnp.float32),
    )
    return (mixed, grad_tokens, grad_gate, grad_w_gate, grad_w_up, grad_w_down)


def solution(mesh):
    in_specs = (
        P("dp", None),
        P("dp", None),
        P("dp"),
        P("dp", "owner"),
        P("dp", "owner"),
        P("owner", "dp"),
        P("dp", "owner"),
    )
    out_specs = (
        P("dp", "owner"),
        P("dp", "owner"),
        P("dp"),
        P("dp", "owner"),
        P("dp", "owner"),
        P("owner", "dp"),
    )
    return jax.shard_map(local, mesh=mesh, in_specs=in_specs, out_specs=out_specs, check_vma=False)
```

profile of v0, /device:TPU:1, one launch (start us, length us, event | category | flops | bytes accessed | tf_op | source)
XLA Modules:
  0.0 644.4 jit_solution(3821113776268114947)
XLA Ops:
  7.2 0.0 all-gather.7.cloned.1.call-start
  7.2 0.7 all-gather.7.cloned.1.call-update
  7.9 0.0 all-gather.5.cloned.1.call-start
  7.9 0.7 all-gather.5.cloned.1.call-update
  8.6 0.0 all-gather.11.cloned.1.call-start
  8.7 0.7 all-gather.11.cloned.1.call-update
  9.4 0.0 all-gather.9.cloned.1.call-start
  9.4 0.5 all-gather.9.cloned.1.call-update
  10.0 0.0 reduce-scatter.14.cloned.1.call-start
  10.0 0.7 compare_reduce_fusion
  10.7 0.3 reduce-window.9
  11.0 0.1 slice.7
  11.1 0.1 slice_reduce_fusion
  11.3 0.1 broadcast_maximum_fusion
  11.3 0.9 select_reduce_fusion
  12.3 5.6 convolution_convert_fusion.3
  17.9 34.0 %all-gather.7.cloned.1.call-done = bf16[4096,384]{1,0:T(8,128)(2,1)} async-done(((bf16[256,384]{1,0:T(8,128)(2,1)}), bf16[4096,384]{1,0:T(8,128)(2,1)}) %all-gather.7.cloned.1.call-update) | async-done | bytes 3145744 | tf_op jit(solution)/shard_map/all_gather | solution.py:28
  51.8 4.6 fusion.15
  56.5 35.2 %all-gather.5.cloned.1.call-done = bf16[4096,384]{1,0:T(8,128)(2,1)} async-done(((bf16[256,384]{1,0:T(8,128)(2,1)}), bf16[4096,384]{1,0:T(8,128)(2,1)}) %all-gather.5.cloned.1.call-update) | async-done | bytes 3145744 | tf_op jit(solution)/shard_map/all_gather | solution.py:27
  91.6 4.6 fusion.14
  96.3 79.0 %all-gather.11.cloned.1.call-done = bf16[512,4096]{1,0:T(8,128)(2,1)} async-done(((bf16[512,256]{1,0:T(8,128)(2,1)}), bf16[512,4096]{1,0:T(8,128)(2,1)}) %all-gather.11.cloned.1.call-update) | async-done | bytes 4194320 | tf_op jit(solution)/shard_map/all_gather | solution.py:50
  175.3 6.6 %fusion.3 = f32[384,4096]{1,0:T(8,128)} fusion(bf16[512,4096]{1,0:T(8,128)(2,1)} %all-gather.11.cloned.1.call-done, s32[512]{0:T(512)S(1)} %get-tuple-element.10, pred[512]{0:T(512)(128)(4,1)S(1)} %get-tuple-element.14), kind=kOutput, calls=%fused_computation.17 | convolution fusion | flops 1611005952 | bytes 10488320 | tf_op jit(solution)/shard_map/dot_general | solution.py:51
  181.9 37.9 %all-gather.9.cloned.1.call-done = bf16[384,4096]{1,0:T(8,128)(2,1)} async-done(((bf16[384,256]{1,0:T(8,128)(2,1)}), bf16[384,4096]{1,0:T(8,128)(2,1)}) %all-gather.9.cloned.1.call-update) | async-done | bytes 3145744 | tf_op jit(solution)/shard_map/all_gather | solution.py:29
  219.8 5.8 multiply_convert_fusion.1
  225.6 0.0 copy-start.3
  225.6 0.0 copy-start.5
  225.7 0.0 copy-done
  225.7 3.6 convolution_convert_fusion
  229.3 0.0 reduce-scatter.14.cloned.1.call-update
  229.3 0.2 reduce-scatter.12.cloned.1.call-start
  229.6 0.0 copy-done.3
  229.6 5.7 convolution_convert_fusion.1
  235.2 0.0 reduce-scatter.12.cloned.1.call-update
  235.3 0.0 reduce-scatter.10.cloned.1.call-start
  235.3 0.0 copy-done.5
  235.3 5.7 convolution_convert_fusion.2
  241.0 0.0 reduce-scatter.10.cloned.1.call-update
  241.0 0.0 reduce-scatter.8.cloned.1.call-start
  241.1 0.1 maximum_bitcast_fusion
  241.2 8.5 %multiply_reduce_fusion = (f32[384]{0:T(512)S(1)}, f32[384,4096]{1,0:T(8,128)}) fusion(f32[384,4096]{1,0:T(8,128)} %fusion.3, bf16[384,384]{1,0:T(8,128)(2,1)S(1)} %get-tuple-element.13, bf16[384,4096]{1,0:T(8,128)(2,1)} %all-gather.9.cloned.1.call-done), kind=kOutput, calls=%fused_computation.7 | convolution fusion | flops 1211104896 | bytes 16025088 | tf_op jit(solution)/shard_map/dot_general | solution.py:45
  249.6 3.5 gather_fusion
  253.1 0.0 copy-done.2
  253.1 0.0 copy-start.1
  253.1 0.0 copy-start.4
  253.2 2.9 fusion.16
  256.1 0.0 copy-done.1
  256.1 0.0 copy-done.4
  256.1 1.8 convolution_add_fusion
  258.0 0.0 copy-start.6
  258.0 4.4 gather_fusion.2
  262.4 5.3 fusion
  267.8 0.0 reduce-scatter.8.cloned.1.call-update
  267.8 0.3 reduce-scatter.6.cloned.1.call-start
  268.1 11.8 %gather_fusion.1 = f32[512,4096]{1,0:T(8,128)} fusion(f32[384,4096]{1,0:T(8,128)} %get-tuple-element.18, s32[1024]{0:T(1024)S(1)} %pad_clamp_fusion.1), kind=kCustom, calls=%fused_computation.clone | custom fusion | bytes 16779264 | tf_op jit(solution)/shard_map/jit(_take)/gather | solution.py:46
  279.8 7.5 %fusion.1 = bf16[512,4096]{1,0:T(8,128)(2,1)} fusion(f32[512,4096]{1,0:T(8,128)} %gather_fusion.1, f32[512]{0:T(512)S(1)} %get-tuple-element.16, pred[512]{0:T(512)(128)(4,1)S(1)} %get-tuple-element.8), kind=kLoop, calls=%fused_computation.6 | loop fusion | flops 6291456 | bytes 12585472 | tf_op jit(solution)/shard_map/convert_element_type | solution.py:48
  287.4 0.0 reduce-scatter.6.cloned.1.call-update
  287.4 38.1 %psum.7 = f32[512]{0:T(512)} all-reduce(f32[512]{0:T(512)S(1)} %get-tuple-element.7), channel_id=1, replica_groups=mesh['dp'=16,'owner'=16] {'owner'}, use_global_device_ids=true, to_apply=%region_6.8 | all-reduce | flops 512 | bytes 4096 | tf_op jit(solution)/shard_map/psum | solution.py:54
  325.5 1.7 convert_element_type.61
  327.2 39.9 %reduce-scatter.12.cloned.1.call-done = bf16[256,384]{1,0:T(8,128)(2,1)} async-done(((bf16[4096,384]{1,0:T(8,128)(2,1)}), bf16[256,384]{1,0:T(8,128)(2,1)}) %reduce-scatter.12.cloned.1.call-update) | async-done | bytes 196624 | tf_op jit(solution)/shard_map/reduce_scatter | solution.py:73
  367.1 1.7 convert_element_type.59
  368.8 69.7 %reduce-scatter.10.cloned.1.call-done = bf16[256,384]{1,0:T(8,128)(2,1)} async-done(((bf16[4096,384]{1,0:T(8,128)(2,1)}), bf16[256,384]{1,0:T(8,128)(2,1)}) %reduce-scatter.10.cloned.1.call-update) | async-done | bytes 196624 | tf_op jit(solution)/shard_map/reduce_scatter | solution.py:70
  438.4 1.7 convert_element_type.57
  440.1 98.8 %reduce-scatter.8.cloned.1.call-done = bf16[512,256]{1,0:T(8,128)(2,1)} async-done(((bf16[512,4096]{1,0:T(8,128)(2,1)}), bf16[512,256]{1,0:T(8,128)(2,1)}) %reduce-scatter.8.cloned.1.call-update) | async-done | bytes 262160 | tf_op jit(solution)/shard_map/reduce_scatter | solution.py:63
  538.9 99.0 %reduce-scatter.6.cloned.1.call-done = bf16[512,256]{1,0:T(8,128)(2,1)} async-done(((bf16[512,4096]{1,0:T(8,128)(2,1)}), bf16[512,256]{1,0:T(8,128)(2,1)}) %reduce-scatter.6.cloned.1.call-update) | async-done | bytes 262160 | tf_op jit(solution)/shard_map/reduce_scatter | solution.py:47
  (8 shorter events, 0.1 us)
Async XLA Ops:
  7.2 44.7 %all-gather.7.cloned.1.call-start = ((), (), s32[]{:S(2)}) async-start(), calls=%async_computation.6 | async-start | bytes 3342336 | tf_op jit(solution)/shard_map/all_gather | solution.py:28
  7.9 83.7 %all-gather.5.cloned.1.call-start = ((), (), s32[]{:S(2)}) async-start(), calls=%async_computation.5 | async-start | bytes 3342336 | tf_op jit(solution)/shard_map/all_gather | solution.py:27
  8.6 166.6 %all-gather.11.cloned.1.call-start = ((), (), s32[]{:S(2)}) async-start(), calls=%async_computation.9 | async-start | bytes 4456448 | tf_op jit(solution)/shard_map/all_gather | solution.py:50
  9.4 210.4 %all-gather.9.cloned.1.call-start = ((), (), s32[]{:S(2)}) async-start(), calls=%async_computation.7 | async-start | bytes 3342336 | tf_op jit(solution)/shard_map/all_gather | solution.py:29
  10.0 315.5 %reduce-scatter.14.cloned.1.call-start = ((), (), s32[]{:S(2)}) async-start(), calls=%async_computation.13 | async-start | bytes 3342336 | tf_op jit(solution)/shard_map/reduce_scatter | solution.py:76
  219.8 5.9 copy-start
  225.6 3.9 copy-start.3
  225.6 9.7 %copy-start.5 = (bf16[384,384]{1,0:T(8,128)(2,1)}, bf16[384,384]{1,0:T(8,128)(2,1)S(1)}, u32[]{:S(2)}) copy-start(bf16[384,384]{1,0:T(8,128)(2,1)S(1)} %get-tuple-element.12) | copy-start | bytes 884740
  229.3 137.8 %reduce-scatter.12.cloned.1.call-start = ((), (), s32[]{:S(2)}) async-start(), calls=%async_computation.12 | async-start | bytes 3342336 | tf_op jit(solution)/shard_map/reduce_scatter | solution.py:73
  235.3 203.2 %reduce-scatter.10.cloned.1.call-start = ((), (), s32[]{:S(2)}) async-start(), calls=%async_computation.11 | async-start | bytes 3342336 | tf_op jit(solution)/shard_map/reduce_scatter | solution.py:70
  241.0 297.9 %reduce-scatter.8.cloned.1.call-start = ((), (), s32[]{:S(2)}) async-start(), calls=%async_computation.10 | async-start | bytes 4456448 | tf_op jit(solution)/shard_map/reduce_scatter | solution.py:63
  241.2 12.0 %copy-start.2 = (bf16[4096,384]{1,0:T(8,128)(2,1)S(1)}, bf16[4096,384]{1,0:T(8,128)(2,1)}, u32[]{:S(2)}) copy-start(bf16[4096,384]{1,0:T(8,128)(2,1)} %all-gather.5.cloned.1.call-done) | copy-start | bytes 9437188
  253.1 3.0 copy-start.1
  253.1 3.0 copy-start.4
  258.0 4.5 copy-start.6
  267.8 370.1 %reduce-scatter.6.cloned.1.call-start = ((), (), s32[]{:S(2)}) async-start(), calls=%async_computation.8 | async-start | bytes 4456448 | tf_op jit(solution)/shard_map/reduce_scatter | solution.py:47
Sparse Core Ops, SparseCore 0:
  9.8 41.9 all-gather.6
  53.7 37.8 all-gather.4
  94.0 81.1 all-gather.10
  176.9 42.8 all-gather.8
  229.4 66.8 reduce-scatter.13
  298.7 68.3 reduce-scatter.11
  369.6 68.7 reduce-scatter.9
  442.6 96.2 reduce-scatter.7
  543.1 94.7 reduce-scatter.5
where the time goes:
time: 645 us; the launch traced here: 644 us
  waiting for transfers between devices  496 us (77%)
  matrix products  55.5 us (9%)
  blocking collectives  38.1 us (6%)
  other arithmetic  20.1 us (3%)
  local copies, waits for them, and re-layouts  19.9 us (3%)
  between operations  14 us (2%)
    reduce_scatter x1, waiting for transfers between devices, local(): lax.psum_scatter(row_terms.astype(jnp.bfloat16), 'owner', scatter_dimensi...  99 us
    reduce_scatter x1, waiting for transfers between devices, local(): lax.psum_scatter(input_terms.astype(jnp.bfloat16), 'owner', scatter_dimen...  98.8 us
    all_gather x1, waiting for transfers between devices, local(): d_full = lax.all_gather(d_out, 'owner', axis=1, tiled=True)  79 us
    reduce_scatter x1, waiting for transfers between devices, local(): lax.psum_scatter(gate_term.astype(jnp.bfloat16), 'dp', scatter_dimension=...  69.7 us
    reduce_scatter x1, waiting for transfers between devices, local(): lax.psum_scatter(up_term.astype(jnp.bfloat16), 'dp', scatter_dimension=0,...  39.9 us
    psum x1, blocking collectives, local(): grad_gate = lax.psum(router_terms, 'owner')  38.1 us
    all_gather x1, waiting for transfers between devices, local(): lax.all_gather(w_down, 'dp', axis=1, tiled=True)  37.9 us
    all_gather x1, waiting for transfers between devices, local(): lax.all_gather(w_gate, 'dp', axis=0, tiled=True)  35.2 us
  transfers between devices with their start and end apart: 9, of which 8 were waited for; matrix products, arithmetic and copies ran while one was open for 13% of the time, Pallas kernels for 0%

commit v1 on v0

v1 whole, which is shorter than its diff:
```python
import functools

import jax
import jax.numpy as jnp
from jax import lax
from jax.experimental import pallas as pl
from jax.experimental.pallas import tpu as pltpu
from jax.sharding import PartitionSpec as P

EXPERTS = 4
MESH = pl.DeviceIdType.MESH
VMEM_LIMIT = 60 * 1024 * 1024


def contract_rows(left, right):
    return lax.dot_general(
        left, right, (((0,), (0,)), ((), ())), preferred_element_type=jnp.float32
    )


def contract_cols(left, right):
    return lax.dot_general(
        left, right, (((1,), (1,)), ((), ())), preferred_element_type=jnp.float32
    )


def place():
    dp = lax.axis_index("dp")
    y, zl, c = dp // 4, (dp // 2) % 2, dp % 2
    return y, zl, c


def slot_of(y, zl, c):
    return (y % 4) * 4 + zl * 2 + c


def enter(targets):
    barrier = pltpu.get_barrier_semaphore()
    for target in targets:
        pl.semaphore_signal(barrier, inc=1, device_id=target, device_id_type=MESH)
    pl.semaphore_wait(barrier, len(targets))


def dp_peers():
    y, zl, c = place()
    return {
        "z": {"dp": slot_of(y, 1 - zl, c)},
        "up": {"dp": slot_of(y + 1, zl, c)},
        "down": {"dp": slot_of(y + 3, zl, c)},
        "sib": {"dp": slot_of(y, zl, 1 - c)},
    }


def gather_kernel(own, full, send_sem, recv_sem):
    y, zl, c = place()
    peers = dp_peers()
    enter(list(peers.values()))
    kinds = own.shape[0]
    mine = slot_of(y, zl, c)

    def send(w, index, slot, peer, src=None):
        copy = pltpu.make_async_remote_copy(
            src_ref=full.at[w, slot] if src is None else src,
            dst_ref=full.at[w, slot],
            send_sem=send_sem.at[w, index],
            recv_sem=recv_sem.at[w, index],
            device_id=peers[peer],
            device_id_type=MESH,
        )
        copy.start()

    def arrived(w, index, slot):
        pltpu.make_async_remote_copy(
            src_ref=full.at[w, slot],
            dst_ref=full.at[w, slot],
            send_sem=send_sem.at[w, index],
            recv_sem=recv_sem.at[w, index],
            device_id=peers["sib"],
            device_id_type=MESH,
        ).wait_recv()

    for w in range(kinds):
        send(w, 0, mine, "z", own.at[w])
        send(w, 1, mine, "up", own.at[w])
        send(w, 2, mine, "down", own.at[w])
        send(w, 3, mine, "sib", own.at[w])
    full[:, pl.ds(mine, 1)] = own[...][:, None]
    for w in range(kinds):
        partner = slot_of(y, 1 - zl, c)
        arrived(w, 0, partner)
        send(w, 4, partner, "up")
        send(w, 5, partner, "down")
        send(w, 6, partner, "sib")
    for w in range(kinds):
        arrived(w, 1, slot_of(y + 3, zl, c))
        arrived(w, 4, slot_of(y + 3, 1 - zl, c))
        send(w, 9, slot_of(y + 3, 0, c), "up")
        arrived(w, 2, slot_of(y + 1, zl, c))
        arrived(w, 5, slot_of(y + 1, 1 - zl, c))
        send(w, 12, slot_of(y + 1, 1, c), "down")
        send(w, 7, slot_of(y + 3, zl, c), "sib")
        send(w, 8, slot_of(y + 3, 1 - zl, c), "sib")
        send(w, 10, slot_of(y + 1, zl, c), "sib")
        send(w, 11, slot_of(y + 1, 1 - zl, c), "sib")
    for w in range(kinds):
        arrived(w, 9, slot_of(y + 2, 0, c))
        send(w, 13, slot_of(y + 2, 0, c), "sib")
        arrived(w, 12, slot_of(y + 2, 1, c))
        send(w, 14, slot_of(y + 2, 1, c), "sib")
    for w in range(kinds):
        for index, slot in (
            (3, slot_of(y, zl, 1 - c)),
            (6, slot_of(y, 1 - zl, 1 - c)),
            (7, slot_of(y + 3, zl, 1 - c)),
            (8, slot_of(y + 3, 1 - zl, 1 - c)),
            (10, slot_of(y + 1, zl, 1 - c)),
            (11, slot_of(y + 1, 1 - zl, 1 - c)),
            (13, slot_of(y + 2, 0, 1 - c)),
            (14, slot_of(y + 2, 1, 1 - c)),
        ):
            arrived(w, index, slot)
    for w in range(kinds):
        for index in range(15):
            pltpu.make_async_remote_copy(
                src_ref=full.at[w, mine],
                dst_ref=full.at[w, mine],
                send_sem=send_sem.at[w, index],
                recv_sem=recv_sem.at[w, index],
                device_id=peers["sib"],
                device_id_type=MESH,
            ).wait_send()


def gather_weights(own):
    kinds, rows, cols = own.shape
    return pl.pallas_call(
        gather_kernel,
        out_shape=jax.ShapeDtypeStruct((kinds, 16, rows, cols), own.dtype),
        in_specs=[pl.BlockSpec(memory_space=pltpu.VMEM)],
        out_specs=pl.BlockSpec(memory_space=pltpu.VMEM),
        scratch_shapes=[
            pltpu.SemaphoreType.DMA((kinds, 15)),
            pltpu.SemaphoreType.DMA((kinds, 15)),
        ],
        compiler_params=pltpu.CompilerParams(
            collective_id=0, has_side_effects=True, vmem_limit_bytes=VMEM_LIMIT
        ),
    )(own)


def add_rows(out, *terms):
    rows = out.shape[0]

    @pl.loop(0, rows // 64)
    def _(step):
        at = pl.ds(pl.multiple_of(step * 64, 64), 64)
        total = terms[0][at, :].astype(jnp.float32)
        for term in terms[1:]:
            total = total + term[at, :].astype(jnp.float32)
        out[at, :] = total.astype(out.dtype)


def reduce_kernel(part, out, sib, first, second, cross, send_sem, recv_sem):
    y, zl, c = place()
    peers = dp_peers()
    enter(list(peers.values()))
    kinds = part.shape[0]

    def copy(w, index, src, dst, peer):
        return pltpu.make_async_remote_copy(
            src_ref=src,
            dst_ref=dst,
            send_sem=send_sem.at[w, index],
            recv_sem=recv_sem.at[w, index],
            device_id=peers[peer],
            device_id_type=MESH,
        )

    order = [(2, 0), (2, 1), (1, 0), (1, 1), (3, 0), (3, 1), (0, 0), (0, 1)]
    for w in range(kinds):
        for index, (dy, half) in enumerate(order):
            copy(
                w, index, part.at[w, slot_of(y + dy, half, 1 - c)], sib.at[w, index], "sib"
            ).start()

    def joined(w, index):
        dy, half = order[index]
        here = part.at[w, slot_of(y + dy, half, c)]
        copy(w, index, sib.at[w, index], sib.at[w, index], "sib").wait_recv()
        return here

    for w in range(kinds):
        for index in (0, 1):
            here = joined(w, index)
            add_rows(sib.at[w, index], sib.at[w, index], here)
            copy(w, 8 + index, sib.at[w, index], first.at[w, index], ("up", "down")[index]).start()
    for w in range(kinds):
        for index in (2, 3, 4, 5):
            here = joined(w, index)
            side, half = (index - 2) // 2, index % 2
            if side == half:
                copy(w, 8 + side, sib.at[w, side], first.at[w, side], "sib").wait_recv()
                add_rows(sib.at[w, index], sib.at[w, index], here, first.at[w, side])
            else:
                add_rows(sib.at[w, index], sib.at[w, index], here)
            copy(w, 8 + index, sib.at[w, index], second.at[w, index - 2], ("up", "down")[side]).start()
    for w in range(kinds):
        for index in (2, 3, 4, 5):
            copy(w, 8 + index, sib.at[w, index], second.at[w, index - 2], "sib").wait_recv()
        for index in (6, 7):
            joined(w, index)
        away = sib.at[w, 6 + 1 - zl]
        add_rows(
            away, away, part.at[w, slot_of(y, 1 - zl, c)], second.at[w, 1 - zl], second.at[w, 3 - zl]
        )
        copy(w, 14, away, cross.at[w], "z").start()
    for w in range(kinds):
        copy(w, 14, cross.at[w], cross.at[w], "z").wait_recv()
        add_rows(
            out.at[w],
            sib.at[w, 6 + zl],
            part.at[w, slot_of(y, zl, c)],
            second.at[w, zl],
            second.at[w, 2 + zl],
            cross.at[w],
        )
    for w in range(kinds):
        for index in range(15):
            copy(w, index, cross.at[w], cross.at[w], "sib").wait_send()


def reduce_weights(part):
    kinds, _, rows, cols = part.shape
    return pl.pallas_call(
        reduce_kernel,
        out_shape=jax.ShapeDtypeStruct((kinds, rows, cols), jnp.float32),
        in_specs=[pl.BlockSpec(memory_space=pltpu.VMEM)],
        out_specs=pl.BlockSpec(memory_space=pltpu.VMEM),
        scratch_shapes=[
            pltpu.VMEM((kinds, 8, rows, cols), part.dtype),
            pltpu.VMEM((kinds, 2, rows, cols), part.dtype),
            pltpu.VMEM((kinds, 4, rows, cols), part.dtype),
            pltpu.VMEM((kinds, rows, cols), part.dtype),
            pltpu.SemaphoreType.DMA((kinds, 15)),
            pltpu.SemaphoreType.DMA((kinds, 15)),
        ],
        compiler_params=pltpu.CompilerParams(
            collective_id=1, has_side_effects=True, vmem_limit_bytes=VMEM_LIMIT
        ),
    )(part)


def local(tokens, route, gate_prob, w_gate, w_up, w_down, d_out):
    row_count = tokens.shape[0]
    capacity = 3 * row_count // 4
    pieces = lax.axis_size("owner") // EXPERTS
    expert = lax.axis_index("owner") // pieces
    d_full = lax.all_gather(d_out, "owner", axis=1, tiled=True)
    full = gather_weights(jnp.stack([w_gate, w_up, w_down.T]))
    width = w_gate.shape[1]
    full_gate, full_up, full_down = (full[i].reshape(-1, width) for i in range(3))
    selected = route[:, 0] == expert
    slot_index = jnp.cumsum(selected.astype(jnp.int32)) - 1
    slot_ids = jnp.arange(capacity, dtype=jnp.int32)
    one_hot = jnp.logical_and(slot_index[None, :] == slot_ids[:, None], selected[None, :])
    dispatch = one_hot.astype(jnp.bfloat16)
    slot_tokens = jnp.dot(dispatch, tokens, preferred_element_type=jnp.float32).astype(jnp.bfloat16)
    slot_probs = jnp.sum(jnp.where(one_hot, gate_prob[None, :], jnp.float32(0.0)), axis=1)
    gate_pre = jnp.dot(slot_tokens, full_gate, preferred_element_type=jnp.float32)
    up_pre = jnp.dot(slot_tokens, full_up, preferred_element_type=jnp.float32)
    sigma = jax.nn.sigmoid(gate_pre)
    active = gate_pre * sigma
    hidden = (active * up_pre).astype(jnp.bfloat16)
    expert_out = contract_cols(hidden, full_down)
    slot_mixed = (expert_out * slot_probs[:, None]).astype(jnp.bfloat16)
    row_terms = contract_rows(dispatch, slot_mixed).astype(jnp.bfloat16)
    mixed = lax.psum_scatter(row_terms, "owner", scatter_dimension=1, tiled=True)
    slot_cotangent = jnp.dot(dispatch, d_full, preferred_element_type=jnp.float32)
    slot_router = jnp.sum(slot_cotangent * expert_out, axis=1)
    router_terms = jnp.sum(jnp.where(one_hot, slot_router[:, None], jnp.float32(0.0)), axis=0)
    grad_gate = lax.psum(router_terms, "owner")
    d_expert = (slot_probs[:, None] * slot_cotangent).astype(jnp.bfloat16)
    d_hidden = jnp.dot(d_expert, full_down, preferred_element_type=jnp.float32)
    d_gate_pre = (d_hidden * up_pre * sigma * (1.0 + gate_pre * (1.0 - sigma))).astype(jnp.bfloat16)
    d_up_pre = (d_hidden * active).astype(jnp.bfloat16)
    slot_input = (contract_cols(d_gate_pre, full_gate) + contract_cols(d_up_pre, full_up)).astype(jnp.bfloat16)
    input_terms = contract_rows(dispatch, slot_input).astype(jnp.bfloat16)
    grad_tokens = lax.psum_scatter(input_terms, "owner", scatter_dimension=1, tiled=True)
    terms = jnp.stack(
        [
            contract_rows(slot_tokens, d_gate_pre).astype(jnp.bfloat16),
            contract_rows(slot_tokens, d_up_pre).astype(jnp.bfloat16),
            contract_rows(d_expert, hidden).astype(jnp.bfloat16),
        ]
    ).reshape(3, 16, -1, width)
    grads = reduce_weights(terms)
    return (mixed, grad_tokens, grad_gate, grads[0], grads[1], grads[2].T)


def solution(mesh):
    in_specs = (
        P("dp", None),
        P("dp", None),
        P("dp"),
        P("dp", "owner"),
        P("dp", "owner"),
        P("owner", "dp"),
        P("dp", "owner"),
    )
    out_specs = (
        P("dp", "owner"),
        P("dp", "owner"),
        P("dp"),
        P("dp", "owner"),
        P("dp", "owner"),
        P("owner", "dp"),
    )
    return jax.shard_map(local, mesh=mesh, in_specs=in_specs, out_specs=out_specs, check_vma=False)
```

time: 645 us -> 313 us (0.49)
  waiting for transfers between devices: 496 us -> 70.3 us
  Pallas kernels: 0 us -> 109 us
  other arithmetic: 20.1 us -> 10.5 us
  local copies, waits for them, and re-layouts: 19.9 us -> 12 us
    reduce_scatter x5 -> x2, waiting for transfers between devices: 307 us -> 55 us  [the longest x1 55 us: local(): lax.psum_scatter(input_terms, 'owner', scatter_dimension=1, tiled=True)]
    pallas_call x0 -> x2, Pallas kernels: none -> 109 us  [the longest x1 57.5 us: reduce_weights(): pl.pallas_call(reduce_kernel, out_shape=jax.ShapeDtypeStruct((kinds, rows...]
    all_gather x3 -> x0, waiting for transfers between devices: 107 us -> none  [the longest x1 37.9 us: local(): lax.all_gather(w_down, 'dp', axis=1, tiled=True)]
    all_gather x1, waiting for transfers between devices: 79 us -> 14.5 us  [local(): d_full = lax.all_gather(d_out, 'owner', axis=1, tiled=True)]
    gather x3 -> x0, local copies, waits for them, and re-layouts: 19.7 us -> none  [the longest x1 11.8 us: local(): row_terms = jnp.take(expert_out, safe_index, axis=0) * row_weights[:, None]]
    convert_element_type x5 -> x0, other arithmetic: 18 us -> none  [the longest x1 7.52 us: local(): row_terms.astype(jnp.bfloat16)]
    dot_general x3 -> x5, matrix products: 15 us -> 25.4 us  [contract_rows(): lax.dot_general(left, right, (((0,), (0,)), ((), ())), preferred_element_...]
    another operation x2 -> x4, other arithmetic: 0.34 us -> 9.41 us  [the longest x1 7.16 us: local(): jnp.stack([contract_rows(slot_tokens, d_gate_pre).astype(jnp.bfloat16), c...]
  transfers between devices with their start and end apart: 9 -> 3, of which waited for: 8 -> 2; matrix products, arithmetic and copies ran while one was open for 13% -> 21% of each run, Pallas kernels for 0% -> 35%
where the time goes in v1:
time: 313 us; the launch traced here: 312 us
  Pallas kernels  109 us (35%)
  waiting for transfers between devices  70.3 us (22%)
  matrix products  58.1 us (19%)
  blocking collectives  38.2 us (12%)
  between operations  13.9 us (4%)
  local copies, waits for them, and re-layouts  12 us (4%)
  other arithmetic  10.5 us (3%)
    pallas_call x1, Pallas kernels, reduce_weights(): pl.pallas_call(reduce_kernel, out_shape=jax.ShapeDtypeStruct((kinds, rows...  57.5 us
    reduce_scatter x1, waiting for transfers between devices, local(): lax.psum_scatter(input_terms, 'owner', scatter_dimension=1, tiled=True)  55 us
    pallas_call x1, Pallas kernels, gather_weights(): pl.pallas_call(gather_kernel, out_shape=jax.ShapeDtypeStruct((kinds, 16,...  51.5 us
    psum x1, blocking collectives, local(): grad_gate = lax.psum(router_terms, 'owner')  38.2 us
    dot_general x5, matrix products, contract_rows(): lax.dot_general(left, right, (((0,), (0,)), ((), ())), preferred_element_...  25.4 us
    all_gather x1, waiting for transfers between devices, local(): d_full = lax.all_gather(d_out, 'owner', axis=1, tiled=True)  14.5 us
    dot_general x2, matrix products, contract_cols(): lax.dot_general(left, right, (((1,), (1,)), ((), ())), preferred_element_...  8.98 us
    dot_general x1, matrix products, local(): jnp.dot(dispatch, d_full, preferred_element_type=jnp.float32)  8.69 us
  transfers between devices with their start and end apart: 3, of which 2 were waited for; matrix products, arithmetic and copies ran while one was open for 21% of the time, Pallas kernels for 35%

profile of v1, /device:TPU:1, one launch (start us, length us, event | category | flops | bytes accessed | tf_op | source)
XLA Modules:
  0.0 312.2 jit_solution(13846275328240274289)
XLA Ops:
  7.2 0.0 all-gather.2.cloned.1.call-start
  7.2 0.7 all-gather.2.cloned.1.call-update
  7.9 0.0 reduce-scatter.3.cloned.1.call-start
  8.0 0.7 compare_reduce_fusion
  8.7 0.3 reduce-window.9
  9.0 0.1 slice.25
  9.1 1.1 copy.17
  10.2 1.9 pad_maximum_fusion.1.own
  12.1 51.5 %shard_map.118 = bf16[3,16,256,384]{3,2,1,0:T(8,128)(2,1)} custom-call(bf16[3,256,384]{2,1,0:T(8,128)(2,1)} %pad_maximum_fusion.1.own), custom_call_target="tpu_custom_call" | custom-call | tf_op jit(solution)/shard_map/pallas_call | solution.py:136
  63.6 0.1 slice_reduce_fusion
  63.7 0.1 add_bitcast_fusion
  63.8 4.0 %convolution_convert_fusion.5 = bf16[384,4096]{1,0:T(8,128)(2,1)S(1)} fusion(bf16[512,4096]{1,0:T(8,128)(2,1)} %param.7, s32[512]{0:T(512)S(1)} %add_bitcast_fusion, pred[512]{0:T(512)(128)(4,1)S(1)} %get-tuple-element.34), kind=kOutput, calls=%fused_computation.10 | convolution fusion | flops 1612578816 | bytes 7342592 | tf_op jit(solution)/shard_map/dot_general | solution.py:267
  67.8 0.0 copy-start.7
  67.8 5.7 %fusion.17 = (bf16[1,16,256,384]{3,2,1,0:T(8,128)(2,1)S(1)}, bf16[1,16,256,384]{3,2,1,0:T(8,128)(2,1)S(1)}, bf16[1,16,256,384]{3,2,1,0:T(8,128)(2,1)S(1)}) fusion(bf16[3,16,256,384]{3,2,1,0:T(8,128)(2,1)} %shard_map.118), kind=kLoop, calls=%fused_computation.39 | loop fusion | bytes 18874368 | tf_op jit(solution)/shard_map/slice | solution.py:261
  73.5 0.0 copy-start.2
  73.5 0.0 copy-start.1
  73.6 1.8 fusion.18
  75.4 0.0 copy-start.6
  75.4 0.0 copy-done.7
  75.4 0.0 copy-done.2
  75.4 2.6 multiply_convert_fusion.5
  78.0 0.0 copy-done.6
  78.0 0.0 copy-done.1
  78.0 4.5 %fusion.19 = f32[384,4096]{1,0:T(8,128)} fusion(bf16[384,384]{1,0:T(8,128)(2,1)S(1)} %get-tuple-element.36, bf16[4096,384]{1,0:T(8,128)(2,1)S(1)} %bitcast.45), kind=kOutput, calls=%fused_computation.41 | convolution fusion | flops 1207959552 | bytes 9732096 | tf_op jit(solution)/shard_map/dot_general | solution.py:22
  82.5 0.0 copy-start.5
  82.5 14.5 %all-gather.2.cloned.1.call-done = bf16[512,4096]{1,0:T(8,128)(2,1)} async-done(((bf16[512,256]{1,0:T(8,128)(2,1)}), bf16[512,4096]{1,0:T(8,128)(2,1)}) %all-gather.2.cloned.1.call-update) | async-done | bytes 4194320 | tf_op jit(solution)/shard_map/all_gather | solution.py:258
  97.0 0.0 copy-start
  97.0 8.7 %multiply_reduce_fusion = (f32[384]{0:T(512)S(1)}, f32[384,4096]{1,0:T(8,128)}) fusion(f32[384,4096]{1,0:T(8,128)} %fusion.19, bf16[512,4096]{1,0:T(8,128)(2,1)} %all-gather.2.cloned.1.call-done, s32[512]{0:T(512)S(1)} %add_bitcast_fusion, pred[512]{0:T(512)(128)(4,1)S(1)} %get-tuple-element.34), kind=kOutput, calls=%fused_computation.1 | convolution fusion | flops 1614151296 | bytes 16781312 | tf_op jit(solution)/shard_map/dot_general | solution.py:278
  105.7 0.0 copy-done.5
  105.7 0.3 select_reduce_fusion
  106.0 0.0 copy-done
  106.1 4.5 %convolution_convert_fusion.1 = bf16[512,4096]{1,0:T(8,128)(2,1)} fusion(f32[384,4096]{1,0:T(8,128)S(1)} %copy-done, f32[384]{0:T(512)S(1)} %get-tuple-element.25, s32[512]{0:T(512)S(1)} %add_bitcast_fusion, pred[512]{0:T(512)(128)(4,1)S(1)} %get-tuple-element.34), kind=kOutput, calls=%fused_computation.6 | convolution fusion | flops 1616248832 | bytes 10489856 | tf_op jit(solution)/shard_map/dot_general | solution.py:16
  110.5 0.0 reduce-scatter.3.cloned.1.call-update
  110.6 0.2 reduce-scatter.5.cloned.1.call-start
  110.8 6.6 %multiply_convert_fusion.3 = (bf16[384,384]{1,0:T(8,128)(2,1)}, bf16[384,384]{1,0:T(8,128)(2,1)S(1)}) fusion(f32[384,384]{1,0:T(8,128)} %copy-done.6, f32[384,384]{1,0:T(8,128)} %get-tuple-element.37, bf16[4096,384]{1,0:T(8,128)(2,1)} %bitcast.46, f32[384,4096]{1,0:T(8,128)} %get-tuple-element.39, f32[384]{0:T(512)S(1)} %get-tuple-element.25), kind=kOutput, calls=%fused_computation.18 | convolution fusion | flops 1213022208 | bytes 11208192 | tf_op jit(solution)/shard_map/dot_general | solution.py:283
  117.4 0.0 copy-start.3
  117.4 4.5 %fusion.20 = f32[384,4096]{1,0:T(8,128)} fusion(bf16[384,384]{1,0:T(8,128)(2,1)S(1)} %get-tuple-element.33, bf16[4096,384]{1,0:T(8,128)(2,1)S(1)} %bitcast.44), kind=kOutput, calls=%fused_computation.42 | convolution fusion | flops 1207959552 | bytes 9732096 | tf_op jit(solution)/shard_map/dot_general | solution.py:22
  121.9 0.0 copy-done.3
  121.9 9.8 %convolution_convert_fusion = bf16[512,4096]{1,0:T(8,128)(2,1)} fusion(f32[384,4096]{1,0:T(8,128)} %fusion.20, bf16[384,384]{1,0:T(8,128)(2,1)} %get-tuple-element.32, bf16[4096,384]{1,0:T(8,128)(2,1)} %bitcast.48, s32[512]{0:T(512)S(1)} %add_bitcast_fusion, pred[512]{0:T(512)(128)(4,1)S(1)} %get-tuple-element.34), kind=kOutput, calls=%fused_computation.5 | convolution fusion | flops 2824208384 | bytes 13928960 | tf_op jit(solution)/shard_map/dot_general | solution.py:16
  131.7 0.0 copy-start.8
  131.7 0.0 reduce-scatter.5.cloned.1.call-update
  131.7 1.9 copy-done.8
  133.6 0.0 copy-start.4
  133.6 0.0 slice-start
  133.6 4.9 %convolution_convert_fusion.3 = bf16[4096,384]{1,0:T(8,128)(2,1)} fusion(bf16[384,4096]{1,0:T(8,128)(2,1)S(1)} %copy-done.8, bf16[384,384]{1,0:T(8,128)(2,1)} %get-tuple-element.32), kind=kOutput, calls=%fused_computation.8 | convolution fusion | flops 1209532416 | bytes 6586368 | tf_op jit(solution)/shard_map/dot_general | solution.py:16
  138.4 0.0 copy-done.4
  138.5 0.0 slice-start.1
  138.5 3.8 %convolution_convert_fusion.4 = bf16[4096,384]{1,0:T(8,128)(2,1)} fusion(bf16[384,4096]{1,0:T(8,128)(2,1)S(1)} %copy-done.8, bf16[384,384]{1,0:T(8,128)(2,1)S(1)} %copy-done.4), kind=kOutput, calls=%fused_computation.9 | convolution fusion | flops 1209532416 | bytes 6586368 | tf_op jit(solution)/shard_map/dot_general | solution.py:16
  142.3 0.0 slice-done
  142.3 0.0 slice-done.1
  142.3 2.5 convolution_convert_fusion.2
  144.8 7.2 %pad_maximum_fusion.part = bf16[3,16,256,384]{3,2,1,0:T(8,128)(2,1)} fusion(bf16[1,16,256,384]{3,2,1,0:T(8,128)(2,1)S(1)} %bitcast.42, bf16[1,16,256,384]{3,2,1,0:T(8,128)(2,1)} %bitcast.49, bf16[1,16,256,384]{3,2,1,0:T(8,128)(2,1)} %bitcast.50), kind=kLoop, calls=%fused_computation | loop fusion | flops 9437184 | bytes 18874368 | tf_op jit(solution)/shard_map/stack | solution.py:289
  152.0 57.5 %shard_map.119 = f32[3,256,384]{2,1,0:T(8,128)} custom-call(bf16[3,16,256,384]{3,2,1,0:T(8,128)(2,1)} %pad_maximum_fusion.part), custom_call_target="tpu_custom_call" | custom-call | tf_op jit(solution)/shard_map/pallas_call | solution.py:234
  209.4 2.2 slice_bitcast_fusion
  211.6 0.9 copy.18
  212.5 38.2 %psum.7 = f32[512]{0:T(512)} all-reduce(f32[512]{0:T(512)S(1)} %get-tuple-element.24), channel_id=1, replica_groups=mesh['dp'=16,'owner'=16] {'owner'}, use_global_device_ids=true, to_apply=%region_7.8 | all-reduce | flops 512 | bytes 4096 | tf_op jit(solution)/shard_map/psum | solution.py:281
  250.7 0.0 reduce-scatter.3.cloned.1.call-done
  250.7 55.0 %reduce-scatter.5.cloned.1.call-done = bf16[512,256]{1,0:T(8,128)(2,1)} async-done(((bf16[512,4096]{1,0:T(8,128)(2,1)}), bf16[512,256]{1,0:T(8,128)(2,1)}) %reduce-scatter.5.cloned.1.call-update) | async-done | bytes 262160 | tf_op jit(solution)/shard_map/reduce_scatter | solution.py:288
  (2 shorter events, 0.0 us)
Async XLA Ops:
  7.2 89.9 %all-gather.2.cloned.1.call-start = ((), (), s32[]{:S(2)}) async-start(), calls=%async_computation.3 | async-start | bytes 4456448 | tf_op jit(solution)/shard_map/all_gather | solution.py:258
  7.9 242.8 %reduce-scatter.3.cloned.1.call-start = ((), (), s32[]{:S(2)}) async-start(), calls=%async_computation.2 | async-start | bytes 4456448 | tf_op jit(solution)/shard_map/reduce_scatter | solution.py:277
  67.8 7.6 %copy-start.7 = (bf16[384,4096]{1,0:T(8,128)(2,1)}, bf16[384,4096]{1,0:T(8,128)(2,1)S(1)}, u32[]{:S(2)}) copy-start(bf16[384,4096]{1,0:T(8,128)(2,1)S(1)} %convolution_convert_fusion.5) | copy-start | bytes 9437188
  73.5 1.9 copy-start.2
  73.5 4.5 %copy-start.1 = (bf16[1,16,256,384]{3,2,1,0:T(8,128)(2,1)}, bf16[1,16,256,384]{3,2,1,0:T(8,128)(2,1)S(1)}, u32[]{:S(2)}) copy-start(bf16[1,16,256,384]{3,2,1,0:T(8,128)(2,1)S(1)} %get-tuple-element.26) | copy-start | bytes 9437188
  75.4 2.6 copy-start.6
  82.5 23.2 %copy-start.5 = (f32[512]{0:T(512)S(1)}, f32[512]{0:T(512)}, u32[]{:S(2)}) copy-start(f32[512]{0:T(512)} %param.9) | copy-start | bytes 6148
  97.0 9.0 %copy-start = (f32[384,4096]{1,0:T(8,128)S(1)}, f32[384,4096]{1,0:T(8,128)}, u32[]{:S(2)}) copy-start(f32[384,4096]{1,0:T(8,128)} %fusion.19) | copy-start | bytes 18874372
  110.6 195.2 %reduce-scatter.5.cloned.1.call-start = ((), (), s32[]{:S(2)}) async-start(), calls=%async_computation.4 | async-start | bytes 4456448 | tf_op jit(solution)/shard_map/reduce_scatter | solution.py:288
  117.4 4.5 %copy-start.3 = (bf16[384,384]{1,0:T(8,128)(2,1)}, bf16[384,384]{1,0:T(8,128)(2,1)S(1)}, u32[]{:S(2)}) copy-start(bf16[384,384]{1,0:T(8,128)(2,1)S(1)} %get-tuple-element.33) | copy-start | bytes 884740
  131.7 1.9 copy-start.8
  133.6 4.9 %copy-start.4 = (bf16[384,384]{1,0:T(8,128)(2,1)S(1)}, bf16[384,384]{1,0:T(8,128)(2,1)}, u32[]{:S(2)}) copy-start(bf16[384,384]{1,0:T(8,128)(2,1)} %copy-done.3) | copy-start | bytes 884740
  133.6 8.7 %slice-start = ((s8[6291456]{0:T(1024)(128)(4,1)}), s8[4194304]{0:T(1024)(128)(4,1)S(1)}, s32[]{:S(2)}) async-start(s8[6291456]{0:T(1024)(128)(4,1)} %bitcast.40), calls=%async_computation.5 | async-start | bytes 8388608
  138.5 3.8 %slice-start.1 = ((s8[6291456]{0:T(1024)(128)(4,1)}), s8[2097152]{0:T(1024)(128)(4,1)S(1)}, s32[]{:S(2)}) async-start(s8[6291456]{0:T(1024)(128)(4,1)} %bitcast.40), calls=%async_computation.6 | async-start | bytes 4194304
Sparse Core Ops, SparseCore 0:
  10.4 86.6 all-gather.1
  110.7 94.9 reduce-scatter.2
  209.9 95.7 reduce-scatter.4

commit v2 on v0

v2 whole, which is shorter than its diff:
```python
import jax
import jax.numpy as jnp
from jax import lax
from jax.experimental import pallas as pl
from jax.experimental.pallas import tpu as pltpu
from jax.sharding import PartitionSpec as P

MESH = pl.DeviceIdType.MESH
VMEM_LIMIT = 63 * 1024 * 1024
BF, F32 = jnp.bfloat16, jnp.float32
CAP, ROWS, CH, PW = 384, 512, 256, 384
COPIES = 120
DOWN = 2


def nn(a, b):
    return lax.dot_general(a, b, (((1,), (0,)), ((), ())), preferred_element_type=F32)


def nt(a, b):
    return lax.dot_general(a, b, (((1,), (1,)), ((), ())), preferred_element_type=F32)


def tn(a, b):
    return lax.dot_general(a, b, (((0,), (0,)), ((), ())), preferred_element_type=F32)


def add_rows(out, *terms):
    rows = out.shape[-2]

    @pl.loop(0, rows // 64)
    def _(step):
        at = pl.ds(pl.multiple_of(step * 64, 64), 64)
        total = terms[0][at, :].astype(F32)
        for term in terms[1:]:
            total = total + term[at, :].astype(F32)
        out[at, :] = total.astype(out.dtype)


def kernel(
    tokens, route, prob, w_gate, w_up, w_down, d_out,
    mixed, grad_tokens, grad_gate, grad_g, grad_u, grad_d,
    full, slots, cot_all, cot, dexp, dhid, dh_a, dh_b, gate, up, hid, dgate, dup,
    part, gt_a, gt_b, m_out, m_in, g_out, g_in,
    grads, sib, first, second, cross, down_t, down_mine, gd_out, gd_in,
    picks, weight, router, r_z, r_x,
    send_sem, recv_sem,
):
    dp, owner = lax.axis_index("dp"), lax.axis_index("owner")
    y, zl, c = dp // 4, (dp // 2) % 2, dp % 2
    zc = dp % 4
    x, zh = owner // 4, owner % 4

    def dp_at(yy, z, cc):
        return (yy % 4) * 4 + z * 2 + cc

    peers = {
        "z": {"dp": dp_at(y, 1 - zl, c)},
        "up": {"dp": dp_at(y + 1, zl, c)},
        "down": {"dp": dp_at(y + 3, zl, c)},
        "sib": {"dp": dp_at(y, zl, 1 - c)},
        "x1": {"owner": ((x + 1) % 4) * 4 + zh},
        "x2": {"owner": ((x + 2) % 4) * 4 + zh},
        "x3": {"owner": ((x + 3) % 4) * 4 + zh},
        "zn": {"owner": x * 4 + (zh + 1) % 4},
        "zp": {"owner": x * 4 + (zh + 3) % 4},
        "z2": {"owner": x * 4 + (zh + 2) % 4},
    }
    turned = {"dp": y * 4 + zh, "owner": x * 4 + zc}
    moved = zh != zc

    barrier = pltpu.get_barrier_semaphore()
    for target in peers.values():
        pl.semaphore_signal(barrier, inc=1, device_id=target, device_id_type=MESH)

    @pl.when(moved)
    def _():
        pl.semaphore_signal(barrier, inc=1, device_id=turned, device_id_type=MESH)

    pl.semaphore_wait(barrier, len(peers) + moved.astype(jnp.int32))

    ids, sent = {}, []

    def index_of(name):
        return ids.setdefault(name, len(ids))

    def describe(name, src, dst, target):
        at = index_of(name)
        return pltpu.make_async_remote_copy(
            src_ref=src,
            dst_ref=dst,
            send_sem=send_sem.at[at],
            recv_sem=recv_sem.at[at],
            device_id=target,
            device_id_type=MESH,
        )

    def send(name, src, dst, peer):
        copy = describe(name, src, dst, peers[peer])
        copy.start()
        sent.append(copy)

    def arrived(name, dst):
        describe(name, dst, dst, peers["sib"]).wait_recv()

    def spread(w, tag, slot, peer, src=None):
        here = full.at[w, slot]
        send(("w", w, tag), here if src is None else src, here, peer)

    def landed(w, tag, slot):
        arrived(("w", w, tag), full.at[w, slot])

    mine = dp_at(y, zl, c)

    def spread0(w, own):
        for tag, peer in ((0, "up"), (1, "down"), (2, "z"), (3, "sib")):
            spread(w, tag, mine, peer, own)

    def spread1(w):
        slot = dp_at(y, 1 - zl, c)
        landed(w, 2, slot)
        for tag, peer in ((4, "up"), (5, "down"), (6, "sib")):
            spread(w, tag, slot, peer)

    def spread2(w):
        landed(w, 0, dp_at(y + 3, zl, c))
        landed(w, 4, dp_at(y + 3, 1 - zl, c))
        spread(w, 9, dp_at(y + 3, 0, c), "up")
        landed(w, 1, dp_at(y + 1, zl, c))
        landed(w, 5, dp_at(y + 1, 1 - zl, c))
        spread(w, 12, dp_at(y + 1, 1, c), "down")
        spread(w, 7, dp_at(y + 3, zl, c), "sib")
        spread(w, 8, dp_at(y + 3, 1 - zl, c), "sib")
        spread(w, 10, dp_at(y + 1, zl, c), "sib")
        spread(w, 11, dp_at(y + 1, 1 - zl, c), "sib")

    def spread3(w):
        landed(w, 9, dp_at(y + 2, 0, c))
        spread(w, 13, dp_at(y + 2, 0, c), "sib")
        landed(w, 12, dp_at(y + 2, 1, c))
        spread(w, 14, dp_at(y + 2, 1, c), "sib")

    def spread4(w):
        o = 1 - c
        for tag, slot in (
            (3, dp_at(y, zl, o)),
            (6, dp_at(y, 1 - zl, o)),
            (7, dp_at(y + 3, zl, o)),
            (8, dp_at(y + 3, 1 - zl, o)),
            (10, dp_at(y + 1, zl, o)),
            (11, dp_at(y + 1, 1 - zl, o)),
            (13, dp_at(y + 2, 0, o)),
            (14, dp_at(y + 2, 1, o)),
        ):
            landed(w, tag, slot)

    def turn(name, src, dst):
        copy = describe(name, src, dst, turned)

        @pl.when(moved)
        def _():
            copy.start()

        return copy

    def turn_wait(copy, src, dst):
        @pl.when(moved)
        def _():
            copy.wait()

        @pl.when(jnp.logical_not(moved))
        def _():
            dst[...] = src[...]

    spread0(0, w_gate)
    down_t[...] = w_down[...].astype(F32).T.astype(BF)
    turn_down = turn("turn_in", down_t, down_mine)
    for step in (1, 3, 2):
        send(("d", step), d_out, cot_all.at[x], "x%d" % step)
    cot_all[x] = d_out[...]
    full[0, mine] = w_gate[...]
    full[1, mine] = w_up[...]

    chosen = route[...]
    is_expert = lax.broadcasted_iota(jnp.int32, (8, ROWS), 0) == chosen
    upto = (
        lax.broadcasted_iota(jnp.int32, (ROWS, ROWS), 0)
        <= lax.broadcasted_iota(jnp.int32, (ROWS, ROWS), 1)
    )
    one, zero = jnp.float32(1.0), jnp.float32(0.0)
    counts = nn(jnp.where(is_expert, one, zero).astype(BF), jnp.where(upto, one, zero).astype(BF))
    place = jnp.where(is_expert, counts.astype(jnp.int32) - 1, -1)
    slot_ids = lax.broadcasted_iota(jnp.int32, (CAP, ROWS), 0)
    for e in range(4):
        picks[e] = jnp.where(slot_ids == place[e : e + 1, :], one, zero).astype(BF)
    pick = picks.at[x]
    weight[...] = jnp.broadcast_to(
        jnp.sum(pick[...].astype(F32) * prob[...], axis=1, keepdims=True), (CAP, 128)
    )

    def token_slots(lo, hi):
        @pl.loop(lo, hi)
        def _(k):
            cols = pl.ds(pl.multiple_of(k * CH, CH), CH)
            slots[k] = nn(pick[...], tokens[:, cols]).astype(BF)

    def project(w, out):
        out[...] = nn(slots[0], full[w, 0])

        @pl.loop(1, 16)
        def _(k):
            out[...] += nn(slots[k], full[w, k])

    spread1(0)
    turn_wait(turn_down, down_t, down_mine)
    spread0(DOWN, down_mine)
    full[DOWN, mine] = down_mine[...]
    token_slots(0, 8)
    spread2(0)
    spread1(DOWN)
    spread0(1, w_up)
    token_slots(8, 16)
    for step in (1, 2, 3):
        arrived(("d", step), cot_all.at[(x + 4 - step) % 4])

    @pl.loop(0, 4)
    def _(i):
        value = nn(pick[...], cot_all[i])
        cot[i] = value.astype(BF)
        dexp[i] = (weight[:, 0:1] * value).astype(BF)

    spread3(0)
    spread4(0)
    spread2(DOWN)
    spread1(1)
    project(0, gate)
    spread3(DOWN)
    spread4(DOWN)

    def hidden_term(p):
        up[...] = nn(dexp[0], full[DOWN, p])

        @pl.loop(1, 4)
        def _(i):
            up[...] += nn(dexp[i], full[DOWN, 4 * i + p])

        dhid[p] = up[...].astype(BF)

    half = CAP // 2
    nxt, prv, far = (zh + 1) % 4, (zh + 3) % 4, (zh + 2) % 4
    hidden_term(far)
    send("h1n", dhid.at[far, pl.ds(0, half)], dh_a.at[0], "zn")
    send("h1p", dhid.at[far, pl.ds(half, half)], dh_a.at[1], "zp")
    hidden_term(nxt)
    spread2(1)
    hidden_term(prv)
    arrived("h1n", dh_a.at[0])
    add_rows(dhid.at[nxt, pl.ds(0, half)], dhid.at[nxt, pl.ds(0, half)], dh_a.at[0])
    send("h2n", dhid.at[nxt], dh_b.at[0], "zn")
    arrived("h1p", dh_a.at[1])
    add_rows(dhid.at[prv, pl.ds(half, half)], dhid.at[prv, pl.ds(half, half)], dh_a.at[1])
    send("h2p", dhid.at[prv], dh_b.at[1], "zp")
    hidden_term(zh)
    spread3(1)
    spread4(1)
    project(1, up)
    arrived("h2n", dh_b.at[0])
    arrived("h2p", dh_b.at[1])

    @pl.loop(0, CAP // 32)
    def _(step):
        at = pl.ds(pl.multiple_of(step * 32, 32), 32)
        g, u = gate[at, :], up[at, :]
        d = dhid[zh, at, :].astype(F32) + dh_b[0, at, :].astype(F32) + dh_b[1, at, :].astype(F32)
        s = jax.nn.sigmoid(g)
        active = g * s
        hid[zh, at, :] = (active * u).astype(BF)
        dgate[at, :] = (d * u * s * (1.0 + g * (1.0 - s))).astype(BF)
        dup[at, :] = (d * active).astype(BF)

    send("a1n", hid.at[zh], hid.at[zh], "zn")
    send("a1p", hid.at[zh], hid.at[zh], "zp")

    def input_term(d):
        @pl.loop(0, 4)
        def _(a):
            k = 4 * a + d
            part[d, a] = (nt(dgate[...], full[0, k]) + nt(dup[...], full[1, k])).astype(BF)

    def grad_term(w, core):
        @pl.loop(0, 8)
        def _(j):
            k = 2 * j + core
            if w == DOWN:
                grads[w, k] = tn(dexp[k // 4], hid[k % 4]).astype(BF)
            else:
                grads[w, k] = tn(slots[k], (dgate if w == 0 else dup)[...]).astype(BF)

    order = [(2, 0), (2, 1), (1, 0), (1, 1), (3, 0), (3, 1), (0, 0), (0, 1)]
    sides = ("up", "down")

    def grad_part(w, index, core):
        dy, z = order[index]
        return grads.at[w, dp_at(y + dy, z, core)]

    def reduce0(w):
        for index in range(8):
            send(("s", w, index), grad_part(w, index, 1 - c), sib.at[w, index], "sib")

    def reduce1(w):
        for index in (0, 1):
            here = sib.at[w, index]
            arrived(("s", w, index), here)
            add_rows(here, here, grad_part(w, index, c))
            send(("t", w, index), here, first.at[w, index], sides[index])

    def reduce2(w):
        for index in (2, 3, 4, 5):
            here = sib.at[w, index]
            arrived(("s", w, index), here)
            side, z = (index - 2) // 2, index % 2
            if side == z:
                arrived(("t", w, side), first.at[w, side])
                add_rows(here, here, grad_part(w, index, c), first.at[w, side])
            else:
                add_rows(here, here, grad_part(w, index, c))
            send(("t", w, index), here, second.at[w, index - 2], sides[side])

    def reduce3(w):
        for index in (2, 3, 4, 5):
            arrived(("t", w, index), second.at[w, index - 2])
        for index in (6, 7):
            arrived(("s", w, index), sib.at[w, index])
        away = sib.at[w, 7 - zl]
        add_rows(
            away,
            away,
            grads.at[w, dp_at(y, 1 - zl, c)],
            second.at[w, 1 - zl],
            second.at[w, 3 - zl],
        )
        send(("c", w), away, cross.at[w], "z")

    def reduce4(w, out):
        arrived(("c", w), cross.at[w])
        add_rows(
            out,
            sib.at[w, 6 + zl],
            grads.at[w, dp_at(y, zl, c)],
            second.at[w, zl],
            second.at[w, 2 + zl],
            cross.at[w],
        )

    input_term(far)
    send("g1n", part.at[far, pl.ds(0, 2)], gt_a.at[0], "zn")
    send("g1p", part.at[far, pl.ds(2, 2)], gt_a.at[1], "zp")
    grad_term(0, 1 - c)
    reduce0(0)
    input_term(nxt)
    input_term(prv)
    arrived("a1n", hid.at[prv])
    send("a2n", hid.at[prv, pl.ds(0, half)], hid.at[prv, pl.ds(0, half)], "zn")
    arrived("a1p", hid.at[nxt])
    send("a2p", hid.at[nxt, pl.ds(half, half)], hid.at[nxt, pl.ds(half, half)], "zp")
    grad_term(0, c)
    reduce1(0)
    arrived("g1n", gt_a.at[0])
    arrived("g1p", gt_a.at[1])
    for a in (0, 1):
        add_rows(part.at[nxt, a], part.at[nxt, a], gt_a.at[0, a])
        add_rows(part.at[prv, a + 2], part.at[prv, a + 2], gt_a.at[1, a])
    send("g2n", part.at[nxt], gt_b.at[0], "zn")
    send("g2p", part.at[prv], gt_b.at[1], "zp")
    grad_term(1, 1 - c)
    reduce0(1)
    grad_term(1, c)
    reduce1(1)
    reduce2(0)
    arrived("a2n", hid.at[far, pl.ds(0, half)])
    arrived("a2p", hid.at[far, pl.ds(half, half)])

    router[...] = jnp.zeros_like(router)

    @pl.loop(0, 4)
    def _(i):
        out = nt(hid[0], full[DOWN, 4 * i])
        for p in range(1, 4):
            out = out + nt(hid[p], full[DOWN, 4 * i + p])
        router[...] += jnp.broadcast_to(
            jnp.sum(cot[i].astype(F32) * out, axis=1, keepdims=True), (CAP, 128)
        )
        m_out[i] = (weight[:, 0:1] * out).astype(BF)

    for step in (1, 3, 2):
        send(("m", step), m_out.at[(x + step) % 4], m_in.at[x], "x%d" % step)
    r_z[zh] = jnp.broadcast_to(
        jnp.sum(pick[...].astype(F32) * router[:, 0:1], axis=0, keepdims=True), (8, ROWS)
    )
    for name in ("zn", "zp", "z2"):
        send(("r", name), r_z.at[zh], r_z.at[zh], name)
    m_in[x] = m_out[x]

    grad_term(DOWN, 1 - c)
    reduce0(DOWN)
    grad_term(DOWN, c)
    reduce2(1)
    reduce1(DOWN)
    input_term(zh)
    reduce3(0)
    for name, q in (("zn", prv), ("zp", nxt), ("z2", far)):
        arrived(("r", name), r_z.at[q])
    r_x[x] = r_z[0] + r_z[1] + r_z[2] + r_z[3]
    for step in (1, 3, 2):
        send(("q", step), r_x.at[x], r_x.at[x], "x%d" % step)
    reduce2(DOWN)
    reduce4(0, grad_g)
    reduce3(1)

    def back_to_rows(source, out):
        total = tn(picks[0], source[0])
        for e in range(1, 4):
            total = total + tn(picks[e], source[e])
        out[...] = total.astype(BF)

    for step in (1, 2, 3):
        arrived(("m", step), m_in.at[(x + 4 - step) % 4])
    back_to_rows(m_in, mixed)
    reduce3(DOWN)
    reduce4(1, grad_u)
    arrived("g2n", gt_b.at[0])
    arrived("g2p", gt_b.at[1])
    for step in (1, 3, 2, 0):
        a = (x + step) % 4
        add_rows(g_out.at[a], part.at[zh, a], gt_b.at[0, a], gt_b.at[1, a])
        if step:
            send(("g", step), g_out.at[a], g_in.at[x], "x%d" % step)
    g_in[x] = g_out[x]
    reduce4(DOWN, gd_out)
    turn_grad = turn("turn_out", gd_out, gd_in)
    for step in (1, 2, 3):
        arrived(("q", step), r_x.at[(x + 4 - step) % 4])
    grad_gate[...] = (r_x[0] + r_x[1] + r_x[2] + r_x[3])[0:1, :]
    turn_wait(turn_grad, gd_out, gd_in)
    grad_d[...] = gd_in[...].astype(F32).T
    for step in (1, 2, 3):
        arrived(("g", step), g_in.at[(x + 4 - step) % 4])
    back_to_rows(g_in, grad_tokens)
    for copy in sent:
        copy.wait_send()


def local(tokens, route, gate_prob, w_gate, w_up, w_down, d_out):
    vmem = pl.BlockSpec(memory_space=pltpu.VMEM)
    weights = (CH, PW)
    square = (CAP, PW)
    block = (CAP, CH)
    mixed, grad_tokens, grad_gate, grad_g, grad_u, grad_d = pl.pallas_call(
        kernel,
        out_shape=(
            jax.ShapeDtypeStruct((ROWS, CH), BF),
            jax.ShapeDtypeStruct((ROWS, CH), BF),
            jax.ShapeDtypeStruct((1, ROWS), F32),
            jax.ShapeDtypeStruct((CH, PW), F32),
            jax.ShapeDtypeStruct((CH, PW), F32),
            jax.ShapeDtypeStruct((PW, CH), F32),
        ),
        in_specs=[vmem] * 7,
        out_specs=(vmem,) * 6,
        scratch_shapes=[
            pltpu.VMEM((3, 16, *weights), BF),
            pltpu.VMEM((16, *block), BF),
            pltpu.VMEM((4, ROWS, CH), BF),
            pltpu.VMEM((4, *block), BF),
            pltpu.VMEM((4, *block), BF),
            pltpu.VMEM((4, *square), BF),
            pltpu.VMEM((2, CAP // 2, PW), BF),
            pltpu.VMEM((2, *square), BF),
            pltpu.VMEM(square, F32),
            pltpu.VMEM(square, F32),
            pltpu.VMEM((4, *square), BF),
            pltpu.VMEM(square, BF),
            pltpu.VMEM(square, BF),
            pltpu.VMEM((4, 4, *block), BF),
            pltpu.VMEM((2, 2, *block), BF),
            pltpu.VMEM((2, 4, *block), BF),
            pltpu.VMEM((4, *block), BF),
            pltpu.VMEM((4, *block), BF),
            pltpu.VMEM((4, *block), BF),
            pltpu.VMEM((4, *block), BF),
            pltpu.VMEM((3, 16, *weights), BF),
            pltpu.VMEM((3, 8, *weights), BF),
            pltpu.VMEM((3, 2, *weights), BF),
            pltpu.VMEM((3, 4, *weights), BF),
            pltpu.VMEM((3, *weights), BF),
            pltpu.VMEM(weights, BF),
            pltpu.VMEM(weights, BF),
            pltpu.VMEM(weights, BF),
            pltpu.VMEM(weights, BF),
            pltpu.VMEM((4, CAP, ROWS), BF),
            pltpu.VMEM((CAP, 128), F32),
            pltpu.VMEM((CAP, 128), F32),
            pltpu.VMEM((4, 8, ROWS), F32),
            pltpu.VMEM((4, 8, ROWS), F32),
            pltpu.SemaphoreType.DMA((COPIES,)),
            pltpu.SemaphoreType.DMA((COPIES,)),
        ],
        compiler_params=pltpu.CompilerParams(
            collective_id=0, has_side_effects=True, vmem_limit_bytes=VMEM_LIMIT
        ),
    )(tokens, route.reshape(1, ROWS), gate_prob.reshape(1, ROWS), w_gate, w_up, w_down, d_out)
    return (mixed, grad_tokens, grad_gate.reshape(ROWS), grad_g, grad_u, grad_d)


def solution(mesh):
    in_specs = (
        P("dp", None),
        P("dp", None),
        P("dp"),
        P("dp", "owner"),
        P("dp", "owner"),
        P("owner", "dp"),
        P("dp", "owner"),
    )
    out_specs = (
        P("dp", "owner"),
        P("dp", "owner"),
        P("dp"),
        P("dp", "owner"),
        P("dp", "owner"),
        P("owner", "dp"),
    )
    return jax.shard_map(local, mesh=mesh, in_specs=in_specs, out_specs=out_specs, check_vma=False)
```

time: 645 us -> 198 us (0.31)
  waiting for transfers between devices: 496 us -> 0 us
  Pallas kernels: 0 us -> 184 us
  matrix products: 55.5 us -> 0 us
  blocking collectives: 38.1 us -> 0 us
  other arithmetic: 20.1 us -> 0 us
  between operations: 14 us -> 0.64 us
  local copies, waits for them, and re-layouts: 19.9 us -> 9.88 us
    reduce_scatter x5 -> x0, waiting for transfers between devices: 307 us -> none  [the longest x1 99 us: local(): lax.psum_scatter(row_terms.astype(jnp.bfloat16), 'owner', scatter_dimensi...]
    all_gather x4 -> x0, waiting for transfers between devices: 186 us -> none  [the longest x1 79 us: local(): d_full = lax.all_gather(d_out, 'owner', axis=1, tiled=True)]
    pallas_call x0 -> x1, Pallas kernels: none -> 184 us  [local(): pl.pallas_call(kernel, out_shape=(jax.ShapeDtypeStruct((ROWS, CH), BF), j...]
    dot_general x11 -> x0, matrix products: 55.5 us -> none  [the longest x3 15 us: contract_rows(): lax.dot_general(left, right, (((0,), (0,)), ((), ())), preferred_element_...]
    psum x1 -> x0, blocking collectives: 38.1 us -> none  [local(): grad_gate = lax.psum(router_terms, 'owner')]
    gather x3 -> x0, local copies, waits for them, and re-layouts: 19.7 us -> none  [the longest x1 11.8 us: local(): row_terms = jnp.take(expert_out, safe_index, axis=0) * row_weights[:, None]]
    convert_element_type x5 -> x0, other arithmetic: 18 us -> none  [the longest x1 7.52 us: local(): row_terms.astype(jnp.bfloat16)]
    unnamed x14 -> x6, local copies, waits for them, and re-layouts: 0.04 us -> 9.88 us
  transfers between devices with their start and end apart: 9 -> 0, of which waited for: 8 -> 0; matrix products, arithmetic and copies ran while one was open for 13% -> 0% of each run, Pallas kernels for 0% -> 0%
where the time goes in v2:
time: 198 us; the launch traced here: 194 us
  Pallas kernels  184 us (93%)
  local copies, waits for them, and re-layouts  9.88 us (5%)
    pallas_call x1, Pallas kernels, local(): pl.pallas_call(kernel, out_shape=(jax.ShapeDtypeStruct((ROWS, CH), BF), j...  184 us
    unnamed x6, local copies, waits for them, and re-layouts  9.88 us

profile of v2, /device:TPU:1, one launch (start us, length us, event | category | flops | bytes accessed | tf_op | source)
XLA Modules:
  0.0 194.3 jit_solution(10993734015786227785)
XLA Ops:
  0.6 183.8 %shard_map.118 = (bf16[512,256]{1,0:T(8,128)(2,1)}, bf16[512,256]{1,0:T(8,128)(2,1)}, f32[1,512]{1,0:T(1,128)}, f32[256,384]{1,0:T(8,128)}, f32[256,384]{1,0:T(8,128)}, /*index=5*/f32[384,256]{1,0:T(8,128)}) custom-call(bf16[512,4096]{1,0:T(8,128)(2,1)} %tokens.1, s32[1,512]{1,0:T(1,128)} %bitcast.3, f32[1,512]{1,0:T(1,128)} %bitcast.4, ...), custom_call_target="tpu_custom_call" | custom-call | tf_op jit(solution)/shard_map/pallas_call | solution.py:458
  184.4 1.7 copy.19
  186.1 1.7 copy.20
  187.7 1.2 copy.21
  189.0 1.8 copy.22
  190.7 1.8 copy.23
  192.5 1.8 copy.24

commit v3 on v2

--- a/solution.py
+++ b/solution.py
@@ -9,7 +9,7 @@
 VMEM_LIMIT = 63 * 1024 * 1024
 BF, F32 = jnp.bfloat16, jnp.float32
 CAP, ROWS, CH, PW = 384, 512, 256, 384
-COPIES = 120
+COPIES = 136
 DOWN = 2
 
 
@@ -41,7 +41,7 @@
     tokens, route, prob, w_gate, w_up, w_down, d_out,
     mixed, grad_tokens, grad_gate, grad_g, grad_u, grad_d,
     full, slots, cot_all, cot, dexp, dhid, dh_a, dh_b, gate, up, hid, dgate, dup,
-    part, gt_a, gt_b, m_out, m_in, g_out, g_in,
+    part, g_in, in_rows, gz_a, gz_b, m_out, m_in,
     grads, sib, first, second, cross, down_t, down_mine, gd_out, gd_in,
     picks, weight, router, r_z, r_x,
     send_sem, recv_sem,
@@ -140,19 +140,12 @@
         landed(w, 12, dp_at(y + 2, 1, c))
         spread(w, 14, dp_at(y + 2, 1, c), "sib")
 
-    def spread4(w):
+    def from_sibling(w, dy):
         o = 1 - c
-        for tag, slot in (
-            (3, dp_at(y, zl, o)),
-            (6, dp_at(y, 1 - zl, o)),
-            (7, dp_at(y + 3, zl, o)),
-            (8, dp_at(y + 3, 1 - zl, o)),
-            (10, dp_at(y + 1, zl, o)),
-            (11, dp_at(y + 1, 1 - zl, o)),
-            (13, dp_at(y + 2, 0, o)),
-            (14, dp_at(y + 2, 1, o)),
-        ):
-            landed(w, tag, slot)
+        tags = {0: (3, 6), 3: (7, 8), 1: (10, 11), 2: (13, 14)}[dy]
+        halves = (0, 1) if dy == 2 else (zl, 1 - zl)
+        for tag, z in zip(tags, halves):
+            landed(w, tag, dp_at(y + dy, z, o))
 
     def turn(name, src, dst):
         copy = describe(name, src, dst, turned)
@@ -204,19 +197,20 @@
             cols = pl.ds(pl.multiple_of(k * CH, CH), CH)
             slots[k] = nn(pick[...], tokens[:, cols]).astype(BF)
 
-    def project(w, out):
-        out[...] = nn(slots[0], full[w, 0])
-
-        @pl.loop(1, 16)
-        def _(k):
-            out[...] += nn(slots[k], full[w, k])
-
-    spread1(0)
+    def project(w, out, dy):
+        base = 4 * ((y + dy) % 4)
+        start = nn(slots[base], full[w, base])
+        out[...] = start if dy == 0 else out[...] + start
+
+        @pl.loop(1, 4)
+        def _(j):
+            out[...] += nn(slots[base + j], full[w, base + j])
+
     turn_wait(turn_down, down_t, down_mine)
     spread0(DOWN, down_mine)
     full[DOWN, mine] = down_mine[...]
+    spread1(0)
     token_slots(0, 8)
-    spread2(0)
     spread1(DOWN)
     spread0(1, w_up)
     token_slots(8, 16)
@@ -229,13 +223,12 @@
         cot[i] = value.astype(BF)
         dexp[i] = (weight[:, 0:1] * value).astype(BF)
 
-    spread3(0)
-    spread4(0)
     spread2(DOWN)
+    spread2(0)
     spread1(1)
-    project(0, gate)
     spread3(DOWN)
-    spread4(DOWN)
+    for dy in range(4):
+        from_sibling(DOWN, dy)
 
     def hidden_term(p):
         up[...] = nn(dexp[0], full[DOWN, p])
@@ -251,8 +244,8 @@
     hidden_term(far)
     send("h1n", dhid.at[far, pl.ds(0, half)], dh_a.at[0], "zn")
     send("h1p", dhid.at[far, pl.ds(half, half)], dh_a.at[1], "zp")
+    spread3(0)
     hidden_term(nxt)
-    spread2(1)
     hidden_term(prv)
     arrived("h1n", dh_a.at[0])
     add_rows(dhid.at[nxt, pl.ds(0, half)], dhid.at[nxt, pl.ds(0, half)], dh_a.at[0])
@@ -261,9 +254,19 @@
     add_rows(dhid.at[prv, pl.ds(half, half)], dhid.at[prv, pl.ds(half, half)], dh_a.at[1])
     send("h2p", dhid.at[prv], dh_b.at[1], "zp")
     hidden_term(zh)
+    for dy in (0, 3):
+        from_sibling(0, dy)
+        project(0, gate, dy)
+    spread2(1)
+    for dy in (1, 2):
+        from_sibling(0, dy)
+        project(0, gate, dy)
+    for dy in (0, 3, 1):
+        from_sibling(1, dy)
+        project(1, up, dy)
     spread3(1)
-    spread4(1)
-    project(1, up)
+    from_sibling(1, 2)
+    project(1, up, 2)
     arrived("h2n", dh_b.at[0])
     arrived("h2p", dh_b.at[1])
 
@@ -286,6 +289,22 @@
         def _(a):
             k = 4 * a + d
             part[d, a] = (nt(dgate[...], full[0, k]) + nt(dup[...], full[1, k])).astype(BF)
+
+    def input_send(tag, d):
+        for step in (2, 1, 3):
+            send(("g", tag, step), part.at[d, (x + step) % 4], g_in.at[d, x], "x%d" % step)
+        g_in[d, x] = part[d, x]
+
+    def back_to_rows(source, out):
+        total = tn(picks[0], source[0])
+        for e in range(1, 4):
+            total = total + tn(picks[e], source[e])
+        out[...] = total.astype(BF)
+
+    def input_rows(tag, d):
+        for step in (1, 3, 2):
+            arrived(("g", tag, step), g_in.at[d, (x + 4 - step) % 4])
+        back_to_rows(g_in.at[d], in_rows.at[d])
 
     def grad_term(w, core):
         @pl.loop(0, 8)
@@ -352,33 +371,46 @@
             cross.at[w],
         )
 
+    rh = ROWS // 2
     input_term(far)
-    send("g1n", part.at[far, pl.ds(0, 2)], gt_a.at[0], "zn")
-    send("g1p", part.at[far, pl.ds(2, 2)], gt_a.at[1], "zp")
+    input_send(0, far)
     grad_term(0, 1 - c)
     reduce0(0)
     input_term(nxt)
-    input_term(prv)
+    input_send(1, nxt)
+    grad_term(0, c)
+    reduce1(0)
     arrived("a1n", hid.at[prv])
     send("a2n", hid.at[prv, pl.ds(0, half)], hid.at[prv, pl.ds(0, half)], "zn")
     arrived("a1p", hid.at[nxt])
     send("a2p", hid.at[nxt, pl.ds(half, half)], hid.at[nxt, pl.ds(half, half)], "zp")
-    grad_term(0, c)
-    reduce1(0)
-    arrived("g1n", gt_a.at[0])
-    arrived("g1p", gt_a.at[1])
-    for a in (0, 1):
-        add_rows(part.at[nxt, a], part.at[nxt, a], gt_a.at[0, a])
-        add_rows(part.at[prv, a + 2], part.at[prv, a + 2], gt_a.at[1, a])
-    send("g2n", part.at[nxt], gt_b.at[0], "zn")
-    send("g2p", part.at[prv], gt_b.at[1], "zp")
+    input_term(prv)
+    input_send(2, prv)
+    input_rows(0, far)
+    send("g1n", in_rows.at[far, pl.ds(0, rh)], gz_a.at[0], "zn")
+    send("g1p", in_rows.at[far, pl.ds(rh, rh)], gz_a.at[1], "zp")
     grad_term(1, 1 - c)
     reduce0(1)
+    reduce2(0)
     grad_term(1, c)
     reduce1(1)
-    reduce2(0)
+    input_term(zh)
+    input_send(3, zh)
+    input_rows(1, nxt)
+    arrived("g1n", gz_a.at[0])
+    add_rows(in_rows.at[nxt, pl.ds(0, rh)], in_rows.at[nxt, pl.ds(0, rh)], gz_a.at[0])
+    send("g2n", in_rows.at[nxt], gz_b.at[0], "zn")
     arrived("a2n", hid.at[far, pl.ds(0, half)])
     arrived("a2p", hid.at[far, pl.ds(half, half)])
+    grad_term(DOWN, 1 - c)
+    reduce0(DOWN)
+    reduce2(1)
+    grad_term(DOWN, c)
+    reduce1(DOWN)
+    input_rows(2, prv)
+    arrived("g1p", gz_a.at[1])
+    add_rows(in_rows.at[prv, pl.ds(rh, rh)], in_rows.at[prv, pl.ds(rh, rh)], gz_a.at[1])
+    send("g2p", in_rows.at[prv], gz_b.at[1], "zp")
 
     router[...] = jnp.zeros_like(router)
 
@@ -401,53 +433,61 @@
         send(("r", name), r_z.at[zh], r_z.at[zh], name)
     m_in[x] = m_out[x]
 
-    grad_term(DOWN, 1 - c)
-    reduce0(DOWN)
-    grad_term(DOWN, c)
-    reduce2(1)
-    reduce1(DOWN)
-    input_term(zh)
     reduce3(0)
+    reduce2(DOWN)
     for name, q in (("zn", prv), ("zp", nxt), ("z2", far)):
         arrived(("r", name), r_z.at[q])
     r_x[x] = r_z[0] + r_z[1] + r_z[2] + r_z[3]
     for step in (1, 3, 2):
         send(("q", step), r_x.at[x], r_x.at[x], "x%d" % step)
-    reduce2(DOWN)
+    reduce3(1)
     reduce4(0, grad_g)
-    reduce3(1)
-
-    def back_to_rows(source, out):
-        total = tn(picks[0], source[0])
-        for e in range(1, 4):
-            total = total + tn(picks[e], source[e])
-        out[...] = total.astype(BF)
-
+    input_rows(3, zh)
+    reduce3(DOWN)
+    reduce4(1, grad_u)
     for step in (1, 2, 3):
         arrived(("m", step), m_in.at[(x + 4 - step) % 4])
     back_to_rows(m_in, mixed)
-    reduce3(DOWN)
-    reduce4(1, grad_u)
-    arrived("g2n", gt_b.at[0])
-    arrived("g2p", gt_b.at[1])
-    for step in (1, 3, 2, 0):
-        a = (x + step) % 4
-        add_rows(g_out.at[a], part.at[zh, a], gt_b.at[0, a], gt_b.at[1, a])
-        if step:
-            send(("g", step), g_out.at[a], g_in.at[x], "x%d" % step)
-    g_in[x] = g_out[x]
     reduce4(DOWN, gd_out)
     turn_grad = turn("turn_out", gd_out, gd_in)
     for step in (1, 2, 3):
         arrived(("q", step), r_x.at[(x + 4 - step) % 4])
     grad_gate[...] = (r_x[0] + r_x[1] + r_x[2] + r_x[3])[0:1, :]
+    arrived("g2n", gz_b.at[0])
+    arrived("g2p", gz_b.at[1])
+    add_rows(grad_tokens, in_rows.at[zh], gz_b.at[0], gz_b.at[1])
     turn_wait(turn_grad, gd_out, gd_in)
     grad_d[...] = gd_in[...].astype(F32).T
-    for step in (1, 2, 3):
-        arrived(("g", step), g_in.at[(x + 4 - step) % 4])
-    back_to_rows(g_in, grad_tokens)
     for copy in sent:
         copy.wait_send()
+
+
+def hand_over(*refs):
+    n = len(refs) // 3
+    ins, outs, sems = refs[:n], refs[n : 2 * n], refs[3 * n]
+    held = refs[2 * n : 3 * n]
+    loads = [pltpu.make_async_copy(ins[i], held[i], sems.at[0, i]) for i in range(n)]
+    stores = [pltpu.make_async_copy(held[i], outs[i], sems.at[1, i]) for i in range(n)]
+    for load in loads:
+        load.start()
+    for load, store in zip(loads, stores):
+        load.wait()
+        store.start()
+    for store in stores:
+        store.wait()
+
+
+def to_outputs(arrays):
+    anywhere = pl.BlockSpec(memory_space=pl.ANY)
+    return pl.pallas_call(
+        hand_over,
+        out_shape=tuple(jax.ShapeDtypeStruct(a.shape, a.dtype) for a in arrays),
+        in_specs=[anywhere] * len(arrays),
+        out_specs=(anywhere,) * len(arrays),
+        scratch_shapes=[pltpu.VMEM(a.shape, a.dtype) for a in arrays]
+        + [pltpu.SemaphoreType.DMA((2, len(arrays)))],
+        compiler_params=pltpu.CompilerParams(vmem_limit_bytes=VMEM_LIMIT),
+    )(*arrays)
 
 
 def local(tokens, route, gate_prob, w_gate, w_up, w_down, d_out):
@@ -455,7 +495,7 @@
     weights = (CH, PW)
     square = (CAP, PW)
     block = (CAP, CH)
-    mixed, grad_tokens, grad_gate, grad_g, grad_u, grad_d = pl.pallas_call(
+    results = pl.pallas_call(
         kernel,
         out_shape=(
             jax.ShapeDtypeStruct((ROWS, CH), BF),
@@ -482,10 +522,10 @@
             pltpu.VMEM(square, BF),
             pltpu.VMEM(square, BF),
             pltpu.VMEM((4, 4, *block), BF),
-            pltpu.VMEM((2, 2, *block), BF),
-            pltpu.VMEM((2, 4, *block), BF),
-            pltpu.VMEM((4, *block), BF),
-            pltpu.VMEM((4, *block), BF),
+            pltpu.VMEM((4, 4, *block), BF),
+            pltpu.VMEM((4, ROWS, CH), BF),
+            pltpu.VMEM((2, ROWS // 2, CH), BF),
+            pltpu.VMEM((2, ROWS, CH), BF),
             pltpu.VMEM((4, *block), BF),
             pltpu.VMEM((4, *block), BF),
             pltpu.VMEM((3, 16, *weights), BF),
@@ -509,6 +549,7 @@
             collective_id=0, has_side_effects=True, vmem_limit_bytes=VMEM_LIMIT
         ),
     )(tokens, route.reshape(1, ROWS), gate_prob.reshape(1, ROWS), w_gate, w_up, w_down, d_out)
+    mixed, grad_tokens, grad_gate, grad_g, grad_u, grad_d = to_outputs(results)
     return (mixed, grad_tokens, grad_gate.reshape(ROWS), grad_g, grad_u, grad_d)
 
 

time: 198 us -> 158 us (0.80); the launches traced: 194 us -> 156 us
  Pallas kernels: 184 us -> 156 us
  local copies, waits for them, and re-layouts: 9.88 us -> 0 us
    pallas_call x1, Pallas kernels: 184 us -> 153 us  [local(): pl.pallas_call(kernel, out_shape=(jax.ShapeDtypeStruct((ROWS, CH), BF), j...]
    unnamed x6 -> x0, local copies, waits for them, and re-layouts: 9.88 us -> none
    pallas_call x0 -> x1, Pallas kernels: none -> 2.27 us  [to_outputs(): pl.pallas_call(hand_over, out_shape=tuple((jax.ShapeDtypeStruct(a.shape,...]
where the time goes in v3:
time: 158 us; the launch traced here: 156 us
  Pallas kernels  156 us (99%)
    pallas_call x1, Pallas kernels, local(): pl.pallas_call(kernel, out_shape=(jax.ShapeDtypeStruct((ROWS, CH), BF), j...  153 us

profile of v3, /device:TPU:1, one launch (start us, length us, event | category | flops | bytes accessed | tf_op | source)
XLA Modules:
  0.0 156.3 jit_solution(18202583496836427081)
XLA Ops:
  0.6 153.4 %shard_map.118 = (bf16[512,256]{1,0:T(8,128)(2,1)}, bf16[512,256]{1,0:T(8,128)(2,1)}, f32[1,512]{1,0:T(1,128)}, f32[256,384]{1,0:T(8,128)}, f32[256,384]{1,0:T(8,128)}, /*index=5*/f32[384,256]{1,0:T(8,128)}) custom-call(bf16[512,4096]{1,0:T(8,128)(2,1)} %tokens.1, s32[1,512]{1,0:T(1,128)} %bitcast.3, f32[1,512]{1,0:T(1,128)} %bitcast.4, ...), custom_call_target="tpu_custom_call" | custom-call | tf_op jit(solution)/shard_map/pallas_call | solution.py:498
  154.0 2.3 %shard_map.119 = (bf16[512,256]{1,0:T(8,128)(2,1)}, bf16[512,256]{1,0:T(8,128)(2,1)}, f32[1,512]{1,0:T(1,128)}, f32[256,384]{1,0:T(8,128)}, f32[256,384]{1,0:T(8,128)}, /*index=5*/f32[384,256]{1,0:T(8,128)}) custom-call(bf16[512,256]{1,0:T(8,128)(2,1)} %get-tuple-element.18.refs_0_, bf16[512,256]{1,0:T(8,128)(2,1)} %get-tuple-element.19.refs_1_, ...), custom_call_target="tpu_custom_call" | custom-call | tf_op jit(solution)/shard_map/pallas_call | solution.py:482

commit v4 on v3

v4 whole, which is shorter than its diff:
```python
import jax
import jax.numpy as jnp
from jax import lax
from jax.experimental import pallas as pl
from jax.experimental.pallas import tpu as pltpu
from jax.sharding import PartitionSpec as P

MESH = pl.DeviceIdType.MESH
VMEM_LIMIT = 63 * 1024 * 1024
BF, F32 = jnp.bfloat16, jnp.float32
CAP, ROWS, CH, PW = 384, 512, 256, 384
COPIES = 236
STAGES = ((0, 256), (256, 128))
DOWN = 2


def nn(a, b):
    return lax.dot_general(a, b, (((1,), (0,)), ((), ())), preferred_element_type=F32)


def nt(a, b):
    return lax.dot_general(a, b, (((1,), (1,)), ((), ())), preferred_element_type=F32)


def add_rows(out, *terms):
    rows = out.shape[-2]

    @pl.loop(0, rows // 64)
    def _(step):
        at = pl.ds(pl.multiple_of(step * 64, 64), 64)
        total = terms[0][at, :].astype(F32)
        for term in terms[1:]:
            total = total + term[at, :].astype(F32)
        out[at, :] = total.astype(out.dtype)


def kernel(
    tokens, route, prob, w_gate, w_up, w_down, d_out,
    mixed, grad_tokens, grad_gate, grad_g, grad_u, grad_d,
    full_a, full_b, slots, cot_all, cot, dexp,
    dhid_a, dhid_b, dh_aa, dh_ab, dh_ba, dh_bb,
    gate_a, gate_b, up_a, up_b, hid_a, hid_b, dgate_a, dgate_b, dup_a, dup_b, acc_a, acc_b,
    part, g_in, in_rows, gz_a, gz_b, m_out, m_in,
    grads_a, grads_b, sib_a, sib_b, first_a, first_b, second_a, second_b, cross_a, cross_b,
    down_t, down_mine, gd_out_a, gd_out_b, gd_in_a, gd_in_b,
    picks, picks_t, slots_t, dexp_t, weight, router, r_z, r_x,
    send_sem, recv_sem,
):
    full, dhid = (full_a, full_b), (dhid_a, dhid_b)
    dh_first, dh_second = (dh_aa, dh_ab), (dh_ba, dh_bb)
    gate, up, hid = (gate_a, gate_b), (up_a, up_b), (hid_a, hid_b)
    dgate, dup, acc = (dgate_a, dgate_b), (dup_a, dup_b), (acc_a, acc_b)
    grads, sib = (grads_a, grads_b), (sib_a, sib_b)
    first, second, cross = (first_a, first_b), (second_a, second_b), (cross_a, cross_b)
    gd_out, gd_in = (gd_out_a, gd_out_b), (gd_in_a, gd_in_b)

    def columns(ref, s):
        return ref.at[:, pl.ds(*STAGES[s])]

    dp, owner = lax.axis_index("dp"), lax.axis_index("owner")
    y, zl, c = dp // 4, (dp // 2) % 2, dp % 2
    zc = dp % 4
    x, zh = owner // 4, owner % 4

    def dp_at(yy, z, cc):
        return (yy % 4) * 4 + z * 2 + cc

    peers = {
        "z": {"dp": dp_at(y, 1 - zl, c)},
        "up": {"dp": dp_at(y + 1, zl, c)},
        "down": {"dp": dp_at(y + 3, zl, c)},
        "sib": {"dp": dp_at(y, zl, 1 - c)},
        "x1": {"owner": ((x + 1) % 4) * 4 + zh},
        "x2": {"owner": ((x + 2) % 4) * 4 + zh},
        "x3": {"owner": ((x + 3) % 4) * 4 + zh},
        "zn": {"owner": x * 4 + (zh + 1) % 4},
        "zp": {"owner": x * 4 + (zh + 3) % 4},
        "z2": {"owner": x * 4 + (zh + 2) % 4},
    }
    turned = {"dp": y * 4 + zh, "owner": x * 4 + zc}
    moved = zh != zc

    barrier = pltpu.get_barrier_semaphore()
    for target in peers.values():
        pl.semaphore_signal(barrier, inc=1, device_id=target, device_id_type=MESH)

    @pl.when(moved)
    def _():
        pl.semaphore_signal(barrier, inc=1, device_id=turned, device_id_type=MESH)

    pl.semaphore_wait(barrier, len(peers) + moved.astype(jnp.int32))

    ids, sent = {}, []

    def index_of(name):
        return ids.setdefault(name, len(ids))

    def describe(name, src, dst, target):
        at = index_of(name)
        return pltpu.make_async_remote_copy(
            src_ref=src,
            dst_ref=dst,
            send_sem=send_sem.at[at],
            recv_sem=recv_sem.at[at],
            device_id=target,
            device_id_type=MESH,
        )

    def send(name, src, dst, peer):
        copy = describe(name, src, dst, peers[peer])
        copy.start()
        sent.append(copy)

    def arrived(name, dst):
        describe(name, dst, dst, peers["sib"]).wait_recv()

    def spread(w, tag, slot, peer, src=None):
        here = full[w[0]].at[w[1], slot]
        send(("w", w, tag), here if src is None else src, here, peer)

    def landed(w, tag, slot):
        arrived(("w", w, tag), full[w[0]].at[w[1], slot])

    mine = dp_at(y, zl, c)

    def spread0(w, own):
        for tag, peer in ((0, "up"), (1, "down"), (2, "z"), (3, "sib")):
            spread(w, tag, mine, peer, columns(own, w[0]))

    def spread1(w):
        slot = dp_at(y, 1 - zl, c)
        landed(w, 2, slot)
        for tag, peer in ((4, "up"), (5, "down"), (6, "sib")):
            spread(w, tag, slot, peer)

    def spread2(w):
        landed(w, 0, dp_at(y + 3, zl, c))
        landed(w, 4, dp_at(y + 3, 1 - zl, c))
        spread(w, 9, dp_at(y + 3, 0, c), "up")
        landed(w, 1, dp_at(y + 1, zl, c))
        landed(w, 5, dp_at(y + 1, 1 - zl, c))
        spread(w, 12, dp_at(y + 1, 1, c), "down")
        spread(w, 7, dp_at(y + 3, zl, c), "sib")
        spread(w, 8, dp_at(y + 3, 1 - zl, c), "sib")
        spread(w, 10, dp_at(y + 1, zl, c), "sib")
        spread(w, 11, dp_at(y + 1, 1 - zl, c), "sib")

    def spread3(w):
        landed(w, 9, dp_at(y + 2, 0, c))
        spread(w, 13, dp_at(y + 2, 0, c), "sib")
        landed(w, 12, dp_at(y + 2, 1, c))
        spread(w, 14, dp_at(y + 2, 1, c), "sib")

    def from_sibling(w, dy):
        o = 1 - c
        tags = {0: (3, 6), 3: (7, 8), 1: (10, 11), 2: (13, 14)}[dy]
        halves = (0, 1) if dy == 2 else (zl, 1 - zl)
        for tag, z in zip(tags, halves):
            landed(w, tag, dp_at(y + dy, z, o))

    def turn(name, src, dst):
        copy = describe(name, src, dst, turned)

        @pl.when(moved)
        def _():
            copy.start()

        return copy

    def turn_wait(copy, src, dst):
        @pl.when(moved)
        def _():
            copy.wait()

        @pl.when(jnp.logical_not(moved))
        def _():
            dst[...] = src[...]

    G1, U1, D1, G2, U2, D2 = [(stage, kind) for stage in (0, 1) for kind in (0, 1, DOWN)]
    spread0(G1, w_gate)
    down_t[...] = w_down[...].astype(F32).T.astype(BF)
    turn_down = turn("turn_in", down_t, down_mine)
    for step in (1, 3, 2):
        send(("d", step), d_out, cot_all.at[x], "x%d" % step)
    cot_all[x] = d_out[...]
    for stage in (0, 1):
        full[stage][0, mine] = columns(w_gate, stage)[...]
        full[stage][1, mine] = columns(w_up, stage)[...]

    chosen = route[...]
    is_expert = lax.broadcasted_iota(jnp.int32, (8, ROWS), 0) == chosen
    upto = (
        lax.broadcasted_iota(jnp.int32, (ROWS, ROWS), 0)
        <= lax.broadcasted_iota(jnp.int32, (ROWS, ROWS), 1)
    )
    one, zero = jnp.float32(1.0), jnp.float32(0.0)
    counts = nn(jnp.where(is_expert, one, zero).astype(BF), jnp.where(upto, one, zero).astype(BF))
    place = jnp.where(is_expert, counts.astype(jnp.int32) - 1, -1)
    slot_ids = lax.broadcasted_iota(jnp.int32, (CAP, ROWS), 0)
    for e in range(4):
        chosen_slots = jnp.where(slot_ids == place[e : e + 1, :], one, zero).astype(BF)
        picks[e] = chosen_slots
        picks_t[e] = chosen_slots.T
    pick = picks.at[x]
    weight[...] = jnp.broadcast_to(
        jnp.sum(pick[...].astype(F32) * prob[...], axis=1, keepdims=True), (CAP, 128)
    )

    def token_slots(lo, hi):
        @pl.loop(lo, hi)
        def _(k):
            cols = pl.ds(pl.multiple_of(k * CH, CH), CH)
            value = nn(pick[...], tokens[:, cols]).astype(BF)
            slots[k] = value
            slots_t[k] = value.T

    def project(w, dy):
        out = (gate, up)[w[1]][w[0]]
        source = full[w[0]]
        base = 4 * ((y + dy) % 4)
        start = nn(slots[base], source[w[1], base])
        out[...] = start if dy == 0 else out[...] + start

        @pl.loop(1, 4)
        def _(j):
            out[...] += nn(slots[base + j], source[w[1], base + j])

    def project_all(w):
        for dy in (0, 3, 1, 2):
            from_sibling(w, dy)
            project(w, dy)

    half = CAP // 2
    nxt, prv, far = (zh + 1) % 4, (zh + 3) % 4, (zh + 2) % 4

    def hidden_term(s, p):
        total = acc[s]
        total[...] = nn(dexp[0], full[s][DOWN, p])

        @pl.loop(1, 4)
        def _(i):
            total[...] += nn(dexp[i], full[s][DOWN, 4 * i + p])

        dhid[s][p] = total[...].astype(BF)

    def hidden0(s):
        hidden_term(s, far)
        send(("h1n", s), dhid[s].at[far, pl.ds(0, half)], dh_first[s].at[0], "zn")
        send(("h1p", s), dhid[s].at[far, pl.ds(half, half)], dh_first[s].at[1], "zp")

    def hidden1(s):
        arrived(("h1n", s), dh_first[s].at[0])
        here = dhid[s].at[nxt, pl.ds(0, half)]
        add_rows(here, here, dh_first[s].at[0])
        send(("h2n", s), dhid[s].at[nxt], dh_second[s].at[0], "zn")
        arrived(("h1p", s), dh_first[s].at[1])
        here = dhid[s].at[prv, pl.ds(half, half)]
        add_rows(here, here, dh_first[s].at[1])
        send(("h2p", s), dhid[s].at[prv], dh_second[s].at[1], "zp")

    def activate(s):
        arrived(("h2n", s), dh_second[s].at[0])
        arrived(("h2p", s), dh_second[s].at[1])

        @pl.loop(0, CAP // 32)
        def _(step):
            at = pl.ds(pl.multiple_of(step * 32, 32), 32)
            g, u = gate[s][at, :], up[s][at, :]
            d = dhid[s][zh, at, :].astype(F32)
            d = d + dh_second[s][0, at, :].astype(F32) + dh_second[s][1, at, :].astype(F32)
            sig = jax.nn.sigmoid(g)
            active = g * sig
            hid[s][zh, at, :] = (active * u).astype(BF)
            dgate[s][at, :] = (d * u * sig * (1.0 + g * (1.0 - sig))).astype(BF)
            dup[s][at, :] = (d * active).astype(BF)

        send(("a1n", s), hid[s].at[zh], hid[s].at[zh], "zn")
        send(("a1p", s), hid[s].at[zh], hid[s].at[zh], "zp")

    def pass_hidden(s):
        arrived(("a1n", s), hid[s].at[prv])
        here = hid[s].at[prv, pl.ds(0, half)]
        send(("a2n", s), here, here, "zn")
        arrived(("a1p", s), hid[s].at[nxt])
        here = hid[s].at[nxt, pl.ds(half, half)]
        send(("a2p", s), here, here, "zp")

    def all_hidden(s):
        arrived(("a2n", s), hid[s].at[far, pl.ds(0, half)])
        arrived(("a2p", s), hid[s].at[far, pl.ds(half, half)])

    def input_term(d):
        @pl.loop(0, 4)
        def _(a):
            k = 4 * a + d
            total = nt(dgate_a[...], full_a[0, k]) + nt(dup_a[...], full_a[1, k])
            total = total + nt(dgate_b[...], full_b[0, k]) + nt(dup_b[...], full_b[1, k])
            part[d, a] = total.astype(BF)

    def input_send(tag, d):
        for step in (2, 1, 3):
            send(("g", tag, step), part.at[d, (x + step) % 4], g_in.at[d, x], "x%d" % step)
        g_in[d, x] = part[d, x]

    def back_to_rows(source, out):
        total = nn(picks_t[0], source[0])
        for e in range(1, 4):
            total = total + nn(picks_t[e], source[e])
        out[...] = total.astype(BF)

    def input_rows(tag, d):
        for step in (1, 3, 2):
            arrived(("g", tag, step), g_in.at[d, (x + 4 - step) % 4])
        back_to_rows(g_in.at[d], in_rows.at[d])

    def grad_term(w, core):
        s, kind = w

        @pl.loop(0, 8)
        def _(j):
            k = 2 * j + core
            if kind == DOWN:
                grads[s][kind, k] = nn(dexp_t[k // 4], hid[s][k % 4]).astype(BF)
            else:
                grads[s][kind, k] = nn(slots_t[k], (dgate, dup)[kind][s][...]).astype(BF)

    order = [(2, 0), (2, 1), (1, 0), (1, 1), (3, 0), (3, 1), (0, 0), (0, 1)]
    sides = ("up", "down")

    def grad_part(w, index, core):
        dy, z = order[index]
        return grads[w[0]].at[w[1], dp_at(y + dy, z, core)]

    def reduce0(w):
        grad_term(w, 1 - c)
        for index in range(8):
            here = sib[w[0]].at[w[1], index]
            send(("s", w, index), grad_part(w, index, 1 - c), here, "sib")

    def reduce1(w):
        grad_term(w, c)
        for index in (0, 1):
            here = sib[w[0]].at[w[1], index]
            arrived(("s", w, index), here)
            add_rows(here, here, grad_part(w, index, c))
            send(("t", w, index), here, first[w[0]].at[w[1], index], sides[index])

    def reduce2(w):
        for index in (2, 3, 4, 5):
            here = sib[w[0]].at[w[1], index]
            arrived(("s", w, index), here)
            side, z = (index - 2) // 2, index % 2
            if side == z:
                came = first[w[0]].at[w[1], side]
                arrived(("t", w, side), came)
                add_rows(here, here, grad_part(w, index, c), came)
            else:
                add_rows(here, here, grad_part(w, index, c))
            send(("t", w, index), here, second[w[0]].at[w[1], index - 2], sides[side])

    def reduce3(w):
        s, kind = w
        for index in (2, 3, 4, 5):
            arrived(("t", w, index), second[s].at[kind, index - 2])
        for index in (6, 7):
            arrived(("s", w, index), sib[s].at[kind, index])
        away = sib[s].at[kind, 7 - zl]
        add_rows(
            away,
            away,
            grads[s].at[kind, dp_at(y, 1 - zl, c)],
            second[s].at[kind, 1 - zl],
            second[s].at[kind, 3 - zl],
        )
        send(("c", w), away, cross[s].at[kind], "z")

    def reduce4(w):
        s, kind = w
        arrived(("c", w), cross[s].at[kind])
        add_rows(
            gd_out[s] if kind == DOWN else columns((grad_g, grad_u)[kind], s),
            sib[s].at[kind, 6 + zl],
            grads[s].at[kind, dp_at(y, zl, c)],
            second[s].at[kind, zl],
            second[s].at[kind, 2 + zl],
            cross[s].at[kind],
        )
        if kind == DOWN:
            return turn(("turn_out", s), gd_out[s], gd_in[s])

    def finish_down(s, copy):
        lo, width = STAGES[s]
        turn_wait(copy, gd_out[s], gd_in[s])
        grad_d[pl.ds(lo, width), :] = gd_in[s][...].astype(F32).T

    def layer_output():
        router[...] = jnp.zeros_like(router)

        @pl.loop(0, 4)
        def _(i):
            out = nt(hid_a[0], full_a[DOWN, 4 * i]) + nt(hid_b[0], full_b[DOWN, 4 * i])
            for p in range(1, 4):
                out = out + nt(hid_a[p], full_a[DOWN, 4 * i + p])
                out = out + nt(hid_b[p], full_b[DOWN, 4 * i + p])
            router[...] += jnp.broadcast_to(
                jnp.sum(cot[i].astype(F32) * out, axis=1, keepdims=True), (CAP, 128)
            )
            m_out[i] = (weight[:, 0:1] * out).astype(BF)

        for step in (1, 3, 2):
            send(("m", step), m_out.at[(x + step) % 4], m_in.at[x], "x%d" % step)
        r_z[zh] = jnp.broadcast_to(
            jnp.sum(pick[...].astype(F32) * router[:, 0:1], axis=0, keepdims=True), (8, ROWS)
        )
        for name in ("zn", "zp", "z2"):
            send(("r", name), r_z.at[zh], r_z.at[zh], name)
        m_in[x] = m_out[x]

    turn_wait(turn_down, down_t, down_mine)
    spread0(D1, down_mine)
    for stage in (0, 1):
        full[stage][DOWN, mine] = columns(down_mine, stage)[...]
    spread1(G1)
    spread0(U1, w_up)
    token_slots(0, 8)
    spread1(D1)
    spread1(U1)
    token_slots(8, 16)
    spread2(D1)
    spread0(D2, down_mine)
    spread2(G1)
    for step in (1, 2, 3):
        arrived(("d", step), cot_all.at[(x + 4 - step) % 4])

    @pl.loop(0, 4)
    def _(i):
        value = nn(pick[...], cot_all[i])
        cot[i] = value.astype(BF)
        scaled = (weight[:, 0:1] * value).astype(BF)
        dexp[i] = scaled
        dexp_t[i] = scaled.T

    spread1(D2)
    spread0(G2, w_gate)
    spread3(D1)
    spread2(U1)
    for dy in range(4):
        from_sibling(D1, dy)
    hidden0(0)
    spread3(G1)
    hidden_term(0, nxt)
    hidden_term(0, prv)
    spread1(G2)
    spread0(U2, w_up)
    spread2(D2)
    spread3(U1)
    hidden1(0)
    project_all(G1)
    hidden_term(0, zh)
    spread1(U2)
    spread2(G2)
    project_all(U1)
    spread3(D2)
    for dy in range(4):
        from_sibling(D2, dy)
    hidden0(1)
    spread2(U2)
    hidden_term(1, nxt)
    hidden_term(1, prv)
    spread3(G2)
    activate(0)
    reduce0(G1)
    spread3(U2)
    reduce1(G1)
    hidden1(1)
    hidden_term(1, zh)
    project_all(G2)
    project_all(U2)
    activate(1)

    rh = ROWS // 2
    input_term(far)
    input_send(0, far)
    pass_hidden(0)
    reduce0(U1)
    input_term(nxt)
    input_send(1, nxt)
    reduce1(U1)
    reduce2(G1)
    pass_hidden(1)
    input_term(prv)
    input_send(2, prv)
    all_hidden(0)
    reduce0(D1)
    input_rows(0, far)
    send("g1n", in_rows.at[far, pl.ds(0, rh)], gz_a.at[0], "zn")
    send("g1p", in_rows.at[far, pl.ds(rh, rh)], gz_a.at[1], "zp")
    reduce1(D1)
    reduce2(U1)
    input_term(zh)
    input_send(3, zh)
    reduce0(G2)
    reduce1(G2)
    reduce0(U2)
    reduce1(U2)
    input_rows(1, nxt)
    arrived("g1n", gz_a.at[0])
    add_rows(in_rows.at[nxt, pl.ds(0, rh)], in_rows.at[nxt, pl.ds(0, rh)], gz_a.at[0])
    send("g2n", in_rows.at[nxt], gz_b.at[0], "zn")
    reduce3(G1)
    reduce2(D1)
    all_hidden(1)
    reduce0(D2)
    reduce1(D2)
    reduce2(G2)
    input_rows(2, prv)
    arrived("g1p", gz_a.at[1])
    add_rows(in_rows.at[prv, pl.ds(rh, rh)], in_rows.at[prv, pl.ds(rh, rh)], gz_a.at[1])
    send("g2p", in_rows.at[prv], gz_b.at[1], "zp")
    reduce3(U1)
    reduce2(U2)
    layer_output()
    reduce4(G1)
    reduce2(D2)
    reduce3(D1)
    reduce4(U1)
    for name, q in (("zn", prv), ("zp", nxt), ("z2", far)):
        arrived(("r", name), r_z.at[q])
    r_x[x] = r_z[0] + r_z[1] + r_z[2] + r_z[3]
    for step in (1, 3, 2):
        send(("q", step), r_x.at[x], r_x.at[x], "x%d" % step)
    reduce3(G2)
    turn_one = reduce4(D1)
    input_rows(3, zh)
    reduce3(U2)
    reduce4(G2)
    reduce3(D2)
    for step in (1, 2, 3):
        arrived(("m", step), m_in.at[(x + 4 - step) % 4])
    back_to_rows(m_in, mixed)
    reduce4(U2)
    turn_two = reduce4(D2)
    finish_down(0, turn_one)
    for step in (1, 2, 3):
        arrived(("q", step), r_x.at[(x + 4 - step) % 4])
    grad_gate[...] = (r_x[0] + r_x[1] + r_x[2] + r_x[3])[0:1, :]
    arrived("g2n", gz_b.at[0])
    arrived("g2p", gz_b.at[1])
    add_rows(grad_tokens, in_rows.at[zh], gz_b.at[0], gz_b.at[1])
    finish_down(1, turn_two)
    for copy in sent:
        copy.wait_send()


def hand_over(*refs):
    n = len(refs) // 3
    ins, outs, sems = refs[:n], refs[n : 2 * n], refs[3 * n]
    held = refs[2 * n : 3 * n]
    loads = [pltpu.make_async_copy(ins[i], held[i], sems.at[0, i]) for i in range(n)]
    stores = [pltpu.make_async_copy(held[i], outs[i], sems.at[1, i]) for i in range(n)]
    for load in loads:
        load.start()
    for load, store in zip(loads, stores):
        load.wait()
        store.start()
    for store in stores:
        store.wait()


def to_outputs(arrays):
    anywhere = pl.BlockSpec(memory_space=pl.ANY)
    return pl.pallas_call(
        hand_over,
        out_shape=tuple(jax.ShapeDtypeStruct(a.shape, a.dtype) for a in arrays),
        in_specs=[anywhere] * len(arrays),
        out_specs=(anywhere,) * len(arrays),
        scratch_shapes=[pltpu.VMEM(a.shape, a.dtype) for a in arrays]
        + [pltpu.SemaphoreType.DMA((2, len(arrays)))],
        compiler_params=pltpu.CompilerParams(vmem_limit_bytes=VMEM_LIMIT),
    )(*arrays)


def local(tokens, route, gate_prob, w_gate, w_up, w_down, d_out):
    vmem = pl.BlockSpec(memory_space=pltpu.VMEM)
    block = (CAP, CH)

    def staged(*shape, dtype=BF):
        return [pltpu.VMEM((*shape, width), dtype) for _, width in STAGES]

    results = pl.pallas_call(
        kernel,
        out_shape=(
            jax.ShapeDtypeStruct((ROWS, CH), BF),
            jax.ShapeDtypeStruct((ROWS, CH), BF),
            jax.ShapeDtypeStruct((1, ROWS), F32),
            jax.ShapeDtypeStruct((CH, PW), F32),
            jax.ShapeDtypeStruct((CH, PW), F32),
            jax.ShapeDtypeStruct((PW, CH), F32),
        ),
        in_specs=[vmem] * 7,
        out_specs=(vmem,) * 6,
        scratch_shapes=[
            *staged(3, 16, CH),
            pltpu.VMEM((16, *block), BF),
            pltpu.VMEM((4, ROWS, CH), BF),
            pltpu.VMEM((4, *block), BF),
            pltpu.VMEM((4, *block), BF),
            *staged(4, CAP),
            *staged(2, CAP // 2),
            *staged(2, CAP),
            *staged(CAP, dtype=F32),
            *staged(CAP, dtype=F32),
            *staged(4, CAP),
            *staged(CAP),
            *staged(CAP),
            *staged(CAP, dtype=F32),
            pltpu.VMEM((4, 4, *block), BF),
            pltpu.VMEM((4, 4, *block), BF),
            pltpu.VMEM((4, ROWS, CH), BF),
            pltpu.VMEM((2, ROWS // 2, CH), BF),
            pltpu.VMEM((2, ROWS, CH), BF),
            pltpu.VMEM((4, *block), BF),
            pltpu.VMEM((4, *block), BF),
            *staged(3, 16, CH),
            *staged(3, 8, CH),
            *staged(3, 2, CH),
            *staged(3, 4, CH),
            *staged(3, CH),
            pltpu.VMEM((CH, PW), BF),
            pltpu.VMEM((CH, PW), BF),
            *staged(CH),
            *staged(CH),
            pltpu.VMEM((4, CAP, ROWS), BF),
            pltpu.VMEM((4, ROWS, CAP), BF),
            pltpu.VMEM((16, CH, CAP), BF),
            pltpu.VMEM((4, CH, CAP), BF),
            pltpu.VMEM((CAP, 128), F32),
            pltpu.VMEM((CAP, 128), F32),
            pltpu.VMEM((4, 8, ROWS), F32),
            pltpu.VMEM((4, 8, ROWS), F32),
            pltpu.SemaphoreType.DMA((COPIES,)),
            pltpu.SemaphoreType.DMA((COPIES,)),
        ],
        compiler_params=pltpu.CompilerParams(
            collective_id=0, has_side_effects=True, vmem_limit_bytes=VMEM_LIMIT
        ),
    )(tokens, route.reshape(1, ROWS), gate_prob.reshape(1, ROWS), w_gate, w_up, w_down, d_out)
    mixed, grad_tokens, grad_gate, grad_g, grad_u, grad_d = to_outputs(results)
    return (mixed, grad_tokens, grad_gate.reshape(ROWS), grad_g, grad_u, grad_d)


def solution(mesh):
    in_specs = (
        P("dp", None),
        P("dp", None),
        P("dp"),
        P("dp", "owner"),
        P("dp", "owner"),
        P("owner", "dp"),
        P("dp", "owner"),
    )
    out_specs = (
        P("dp", "owner"),
        P("dp", "owner"),
        P("dp"),
        P("dp", "owner"),
        P("dp", "owner"),
        P("owner", "dp"),
    )
    return jax.shard_map(local, mesh=mesh, in_specs=in_specs, out_specs=out_specs, check_vma=False)
```

time: 158 us -> 148 us (0.937)
  Pallas kernels: 156 us -> 147 us
    pallas_call x1, Pallas kernels: 153 us -> 145 us  [local(): pl.pallas_call(kernel, out_shape=(jax.ShapeDtypeStruct((ROWS, CH), BF), j...]
where the time goes in v4:
time: 148 us
  Pallas kernels  147 us (99%)
    pallas_call x1, Pallas kernels, local(): pl.pallas_call(kernel, out_shape=(jax.ShapeDtypeStruct((ROWS, CH), BF), j...  145 us

profile of v4, /device:TPU:1, one launch (start us, length us, event | category | flops | bytes accessed | tf_op | source)
XLA Modules:
  0.0 147.8 jit_solution(9744520512301144044)
XLA Ops:
  0.6 144.8 %shard_map.118 = (bf16[512,256]{1,0:T(8,128)(2,1)}, bf16[512,256]{1,0:T(8,128)(2,1)}, f32[1,512]{1,0:T(1,128)}, f32[256,384]{1,0:T(8,128)}, f32[256,384]{1,0:T(8,128)}, /*index=5*/f32[384,256]{1,0:T(8,128)}) custom-call(bf16[512,4096]{1,0:T(8,128)(2,1)} %tokens.1, s32[1,512]{1,0:T(1,128)} %bitcast.3, f32[1,512]{1,0:T(1,128)} %bitcast.4, ...), custom_call_target="tpu_custom_call" | custom-call | tf_op jit(solution)/shard_map/pallas_call | solution.py:590
  145.5 2.3 %shard_map.119 = (bf16[512,256]{1,0:T(8,128)(2,1)}, bf16[512,256]{1,0:T(8,128)(2,1)}, f32[1,512]{1,0:T(1,128)}, f32[256,384]{1,0:T(8,128)}, f32[256,384]{1,0:T(8,128)}, /*index=5*/f32[384,256]{1,0:T(8,128)}) custom-call(bf16[512,256]{1,0:T(8,128)(2,1)} %get-tuple-element.18.refs_0_, bf16[512,256]{1,0:T(8,128)(2,1)} %get-tuple-element.19.refs_1_, ...), custom_call_target="tpu_custom_call" | custom-call | tf_op jit(solution)/shard_map/pallas_call | solution.py:572

commit v5 on v4

--- a/solution.py
+++ b/solution.py
@@ -35,7 +35,7 @@
 
 
 def kernel(
-    tokens, route, prob, w_gate, w_up, w_down, d_out,
+    tokens_hbm, route, prob, w_gate, w_up, w_down, d_out,
     mixed, grad_tokens, grad_gate, grad_g, grad_u, grad_d,
     full_a, full_b, slots, cot_all, cot, dexp,
     dhid_a, dhid_b, dh_aa, dh_ab, dh_ba, dh_bb,
@@ -44,7 +44,7 @@
     grads_a, grads_b, sib_a, sib_b, first_a, first_b, second_a, second_b, cross_a, cross_b,
     down_t, down_mine, gd_out_a, gd_out_b, gd_in_a, gd_in_b,
     picks, picks_t, slots_t, dexp_t, weight, router, r_z, r_x,
-    send_sem, recv_sem,
+    tokens, tokens_sem, send_sem, recv_sem,
 ):
     full, dhid = (full_a, full_b), (dhid_a, dhid_b)
     dh_first, dh_second = (dh_aa, dh_ab), (dh_ba, dh_bb)
@@ -80,6 +80,8 @@
     turned = {"dp": y * 4 + zh, "owner": x * 4 + zc}
     moved = zh != zc
 
+    load_tokens = pltpu.make_async_copy(tokens_hbm, tokens, tokens_sem)
+    load_tokens.start()
     barrier = pltpu.get_barrier_semaphore()
     for target in peers.values():
         pl.semaphore_signal(barrier, inc=1, device_id=target, device_id_type=MESH)
@@ -88,6 +90,7 @@
     def _():
         pl.semaphore_signal(barrier, inc=1, device_id=turned, device_id_type=MESH)
 
+    down_t[...] = w_down[...].astype(F32).T.astype(BF)
     pl.semaphore_wait(barrier, len(peers) + moved.astype(jnp.int32))
 
     ids, sent = {}, []
@@ -178,7 +181,6 @@
 
     G1, U1, D1, G2, U2, D2 = [(stage, kind) for stage in (0, 1) for kind in (0, 1, DOWN)]
     spread0(G1, w_gate)
-    down_t[...] = w_down[...].astype(F32).T.astype(BF)
     turn_down = turn("turn_in", down_t, down_mine)
     for step in (1, 3, 2):
         send(("d", step), d_out, cot_all.at[x], "x%d" % step)
@@ -422,6 +424,7 @@
         full[stage][DOWN, mine] = columns(down_mine, stage)[...]
     spread1(G1)
     spread0(U1, w_up)
+    load_tokens.wait()
     token_slots(0, 8)
     spread1(D1)
     spread1(U1)
@@ -597,7 +600,7 @@
             jax.ShapeDtypeStruct((CH, PW), F32),
             jax.ShapeDtypeStruct((PW, CH), F32),
         ),
-        in_specs=[vmem] * 7,
+        in_specs=[pl.BlockSpec(memory_space=pl.ANY)] + [vmem] * 6,
         out_specs=(vmem,) * 6,
         scratch_shapes=[
             *staged(3, 16, CH),
@@ -638,6 +641,8 @@
             pltpu.VMEM((CAP, 128), F32),
             pltpu.VMEM((4, 8, ROWS), F32),
             pltpu.VMEM((4, 8, ROWS), F32),
+            pltpu.VMEM((ROWS, 16 * CH), BF),
+            pltpu.SemaphoreType.DMA,
             pltpu.SemaphoreType.DMA((COPIES,)),
             pltpu.SemaphoreType.DMA((COPIES,)),
         ],

time: 148 us -> 147 us (level)
  Pallas kernels: 147 us -> 145 us
    pallas_call x1, Pallas kernels: 145 us -> 143 us  [local(): pl.pallas_call(kernel, out_shape=(jax.ShapeDtypeStruct((ROWS, CH), BF), j...]
where the time goes in v5:
time: 147 us; the launch traced here: 146 us
  Pallas kernels  145 us (99%)
    pallas_call x1, Pallas kernels, local(): pl.pallas_call(kernel, out_shape=(jax.ShapeDtypeStruct((ROWS, CH), BF), j...  143 us

profile of v5, /device:TPU:1, one launch (start us, length us, event | category | flops | bytes accessed | tf_op | source)
XLA Modules:
  0.0 145.6 jit_solution(1391624275244912514)
XLA Ops:
  0.6 142.7 %shard_map.118 = (bf16[512,256]{1,0:T(8,128)(2,1)}, bf16[512,256]{1,0:T(8,128)(2,1)}, f32[1,512]{1,0:T(1,128)}, f32[256,384]{1,0:T(8,128)}, f32[256,384]{1,0:T(8,128)}, /*index=5*/f32[384,256]{1,0:T(8,128)}) custom-call(bf16[512,4096]{1,0:T(8,128)(2,1)} %tokens_hbm.1, s32[1,512]{1,0:T(1,128)} %bitcast.3, f32[1,512]{1,0:T(1,128)} %bitcast.4, ...), custom_call_target="tpu_custom_call" | custom-call | tf_op jit(solution)/shard_map/pallas_call | solution.py:593
  143.4 2.3 %shard_map.119 = (bf16[512,256]{1,0:T(8,128)(2,1)}, bf16[512,256]{1,0:T(8,128)(2,1)}, f32[1,512]{1,0:T(1,128)}, f32[256,384]{1,0:T(8,128)}, f32[256,384]{1,0:T(8,128)}, /*index=5*/f32[384,256]{1,0:T(8,128)}) custom-call(bf16[512,256]{1,0:T(8,128)(2,1)} %get-tuple-element.18.refs_0_, bf16[512,256]{1,0:T(8,128)(2,1)} %get-tuple-element.19.refs_1_, ...), custom_call_target="tpu_custom_call" | custom-call | tf_op jit(solution)/shard_map/pallas_call | solution.py:575
